TPU v7x, 256 devices: a whole 4x4x8 slice. The times are simulated.
256 devices in a mesh: win: 16 (over z_hi, y), tmpl: 16 (over z_lo, x, core).
Axes of the slice: x: 4, y: 4, z: 8 (z_hi: 4, z_lo: 2; z = z_hi * 2 + z_lo), core: 2. Of those that a mesh axis runs over, the one named last changes fastest.
Arguments:
- raw: bfloat16 [4096, 32768], P(('win', 'tmpl')), may hold values from -160 to 160
- ids: int32 [4096], replicated, may hold values from -1 to 2447, as said below
- fir: bfloat16 [64], replicated, may hold values from -0.75 to 0.75
- taps: bfloat16 [2048, 30, 400], P('tmpl'), may hold values from -0.3125 to 0.3125
- channels: int32 [2048, 30], P('tmpl'), may hold values from 0 to 2447, all different within a row
- shifts: int32 [2048, 30], P('tmpl'), may hold values from 0 to 255
Outputs:
- stack: float32 [2048, 16384], P('tmpl', 'win')
Inputs may be any that keep to these rules, and one draw needn't show every extreme that they name: `ids`: each station channel 0 to 2447 stands in exactly one slot, the others hold -1; the owners of one index of tmpl hold exactly 153 live slots together, and one owner of each holds 16 live slots. Each template names 30 different channels; every channel is named by some template.
All inputs are finite; a program needn't handle non-finite values.
Results may differ from a plain program's by a relative error of at most 0.007.
Values may be sent and summed in bfloat16 or wider, within the bound.
A program may use at most 128 MiB of HBM per device.

v0:
```python
import math

import jax
import jax.numpy as jnp
from jax import lax
from jax.sharding import PartitionSpec as P

WIN_DEV = 1024
MARGIN = 768
TL = 400
CH = 30
DEC = 2
NTAP = 64
NS = 1792
NF = 896


def passed_along(shard, axis, by):
    devices = lax.axis_size(axis)
    pairs = [(i, i + by) for i in range(devices) if 0 <= i + by < devices]
    return lax.ppermute(shard, axis, pairs)


def band_matrix(fir, block):
    in_index = jnp.arange(DEC * block + NTAP, dtype=jnp.int32)[:, None]
    out_index = jnp.arange(block, dtype=jnp.int32)[None, :]
    offset = in_index - DEC * out_index
    onehot = offset[:, :, None] == jnp.arange(NTAP, dtype=jnp.int32)[None, None, :]
    values = jnp.where(onehot, fir.astype(jnp.float32)[None, None, :], jnp.float32(0.0))
    return jnp.sum(values, axis=2).astype(jnp.bfloat16)


def decimate(raw_ext, fir, count):
    block = math.gcd(count, 128)
    pieces = count // block
    length = DEC * block
    height = raw_ext.shape[0]
    padded = jnp.pad(raw_ext, ((0, 0), (0, (pieces + 1) * length - raw_ext.shape[1])))
    blocks = padded.reshape(height, pieces + 1, length)
    segments = jnp.concatenate([blocks[:, :pieces], blocks[:, 1:, :NTAP]], axis=2)
    band = band_matrix(fir, block)
    result = jnp.einsum("rbi,in->rbn", segments, band, preferred_element_type=jnp.float32)
    return result.reshape(height, count)


def forward_table():
    sample_index = jnp.arange(NS, dtype=jnp.int32)[:, None]
    frequency = jnp.arange(NF, dtype=jnp.int32)[None, :]
    angle = (sample_index * frequency % NS).astype(jnp.float32) * jnp.float32(2.0 * math.pi / NS)
    return jnp.concatenate([jnp.cos(angle), jnp.sin(angle)], axis=1).astype(jnp.bfloat16)


def inverse_table():
    frequency = jnp.arange(NF, dtype=jnp.int32)[:, None]
    time_index = jnp.arange(WIN_DEV, dtype=jnp.int32)[None, :]
    angle = (frequency * time_index % NS).astype(jnp.float32) * jnp.float32(2.0 * math.pi / NS)
    return jnp.concatenate([jnp.cos(angle), -jnp.sin(angle)], axis=0).astype(jnp.bfloat16)


def spectra(tiles, table):
    values = tiles.astype(jnp.float32)
    scale = lax.rsqrt(jnp.mean(values * values, axis=1, keepdims=True) + 1e-05)
    return (jnp.dot(tiles, table, preferred_element_type=jnp.float32) * scale).astype(jnp.bfloat16)


def stack_block(template_spec, data_spec, shift_block, inverse):
    tmpl_cos = template_spec[:, :NF].astype(jnp.float32)
    tmpl_sin = template_spec[:, NF:].astype(jnp.float32)
    data_cos = data_spec[:, :NF].astype(jnp.float32)
    data_sin = data_spec[:, NF:].astype(jnp.float32)
    real_part = tmpl_cos * data_cos + tmpl_sin * data_sin
    imag_part = tmpl_sin * data_cos - tmpl_cos * data_sin
    frequency = jnp.arange(NF, dtype=jnp.int32)[None, :]
    angle = (shift_block[:, None] * frequency % NS).astype(jnp.float32) * jnp.float32(
        2.0 * math.pi / NS
    )
    phase_cos = jnp.cos(angle)
    phase_sin = jnp.sin(angle)
    rotated_real = real_part * phase_cos - imag_part * phase_sin
    rotated_imag = real_part * phase_sin + imag_part * phase_cos
    group = shift_block.shape[0] // CH
    summed_real = jnp.sum(rotated_real.reshape(group, CH, NF), axis=1)
    summed_imag = jnp.sum(rotated_imag.reshape(group, CH, NF), axis=1)
    weight = jnp.where(jnp.arange(NF) == 0, 1.0, 2.0).astype(jnp.float32) / jnp.float32(CH * NS)
    packed = jnp.concatenate([summed_real * weight, summed_imag * weight], axis=1).astype(
        jnp.bfloat16
    )
    return jnp.dot(packed, inverse, preferred_element_type=jnp.float32)


def on_device(raw, ids, fir, taps, channels, shifts):
    win_count = lax.axis_size("win")
    tmpl_count = lax.axis_size("tmpl")
    slot_count = raw.shape[0]
    live_col = 3 * slot_count * win_count // 5
    chan_total = live_col * tmpl_count
    local_raw = lax.all_to_all(raw, "win", split_axis=1, concat_axis=0, tiled=True)
    extra = DEC * MARGIN + NTAP
    margin = passed_along(local_raw[:, :extra], "win", -1)
    tiles = decimate(jnp.concatenate([local_raw, margin], axis=1), fir, NS).astype(jnp.bfloat16)
    forward = forward_table()
    inverse = inverse_table()
    local_spec = spectra(tiles, forward)
    grid = (
        ids.reshape(win_count, tmpl_count, slot_count)
        .transpose(1, 0, 2)
        .reshape(tmpl_count, win_count * slot_count)
    )
    gathered = lax.all_gather(local_spec, "tmpl", axis=0, tiled=True)
    labels = grid.reshape(-1)
    position = jnp.arange(labels.shape[0], dtype=jnp.int32)
    keyed = jnp.where(labels >= 0, labels, chan_total + position)
    row_of = jnp.argsort(keyed)[:chan_total]
    flat_taps = taps.reshape(-1, TL)
    head = forward[:TL]
    template_spec = jnp.dot(flat_taps, head, preferred_element_type=jnp.float32).astype(
        jnp.bfloat16
    )
    data_rows = jnp.take(row_of, channels.reshape(-1))
    data_all = lax.optimization_barrier(jnp.take(gathered, data_rows, axis=0))
    flat_shifts = shifts.reshape(-1)
    templates_here = taps.shape[0]
    group = math.gcd(templates_here, 32)
    count = templates_here // group

    def one_block(block_index):
        start = block_index * group * CH
        spec_block = lax.dynamic_slice_in_dim(template_spec, start, group * CH, 0)
        data_spec = lax.dynamic_slice_in_dim(data_all, start, group * CH, 0)
        shift_block = lax.dynamic_slice_in_dim(flat_shifts, start, group * CH, 0)
        return stack_block(spec_block, data_spec, shift_block, inverse)

    result = lax.map(one_block, jnp.arange(count, dtype=jnp.int32))
    return result.reshape(templates_here, WIN_DEV)


def solution(mesh):
    return jax.shard_map(
        on_device,
        mesh=mesh,
        in_specs=(
            P(("win", "tmpl"), None),
            P(),
            P(),
            P("tmpl", None, None),
            P("tmpl", None),
            P("tmpl", None),
        ),
        out_specs=P("tmpl", "win"),
        check_vma=False,
    )
```

profile of v0, /device:TPU:89, one launch (start us, length us, event | category | flops | bytes accessed | tf_op | source)
XLA Modules:
  0.0 396.4 jit_solution(3361281532618030527)
XLA Ops:
  8.9 9.9 %all-to-all-start = ((bf16[16,16,2048]{2,0,1:T(8,128)(2,1)}), bf16[16,16,2048]{2,0,1:T(8,128)(2,1)S(1)}, u32[]{:S(2)}, u32[]{:S(2)}) async-start(bf16[16,16,2048]{2,0,1:T(8,128)(2,1)} %bitcast.25), calls=%async_computation | async-start | bytes 2097152 | tf_op jit(solution)/shard_map/all_to_all | solution.py:97
  18.8 26.8 %all-to-all-done = bf16[16,16,2048]{2,0,1:T(8,128)(2,1)S(1)} async-done(((bf16[16,16,2048]{2,0,1:T(8,128)(2,1)}), bf16[16,16,2048]{2,0,1:T(8,128)(2,1)S(1)}, u32[]{:S(2)}, u32[]{:S(2)}) %all-to-all-start) | async-done | bytes 1048608 | tf_op jit(solution)/shard_map/all_to_all | solution.py:97
  49.1 3.7 select_reduce_fusion
  52.8 28.3 %sine_convert_fusion = (bf16[1792,896]{1,0:T(8,128)(2,1)}, bf16[1792,896]{1,0:T(8,128)(2,1)}) fusion(), kind=kLoop, calls=%fused_computation.41 | loop fusion | flops 17661952 | bytes 6422528 | tf_op jit(solution)/shard_map/convert.5
  81.1 7.5 %collective-permute-done = bf16[256,1600]{0,1:T(8,128)(2,1)S(1)} collective-permute-done((bf16[256,1600]{0,1:T(8,128)(2,1)S(1)}, bf16[256,1600]{0,1:T(8,128)(2,1)S(1)}, u32[]{:S(2)}, u32[]{:S(2)}) %collective-permute-start) | collective-permute-done | bytes 819232 | tf_op jit(solution)/shard_map/ppermute | solution.py:21
  98.3 4.1 %fusion.32 = bf16[256,1792]{1,0:T(8,128)(2,1)} fusion(bf16[256,1792]{0,1:T(8,128)(2,1)S(1)} %bitcast.38, bf16[1792,896]{1,0:T(8,128)(2,1)S(1)} %copy-done, bf16[1792,896]{1,0:T(8,128)(2,1)S(1)} %copy-done.1, f32[256]{0:T(256)S(1)} %add_rsqrt_fusion), kind=kOutput, calls=%fused_computation.58 | convolution fusion | flops 1657929728 | bytes 8258560 | tf_op jit(solution)/shard_map/dot_general | solution.py:63
  103.1 5.8 %sort.17 = (s32[4096]{0:T(1024)}, s32[4096]{0:T(1024)S(1)}) sort(s32[4096]{0:T(1024)S(1)} %compare_select_fusion.3, s32[4096]{0:T(1024)S(1)} %iota.62), dimensions={0}, to_apply=%region_0.1 | sort | flops 49152 | bytes 65536 | tf_op jit(solution)/shard_map/jit(argsort)/sort | solution.py:113
  108.9 7.9 %copy.33 = bf16[128,30,400]{2,1,0:T(8,128)(2,1)} copy(bf16[128,30,400]{0,2,1:T(8,128)(2,1)} %param.11) | data formatting | bytes 6144000 | tf_op args[3]
  116.8 7.0 %reshape.155 = bf16[3840,400]{1,0:T(8,128)(2,1)} reshape(bf16[128,30,400]{2,1,0:T(8,128)(2,1)} %copy.33) | data formatting | bytes 6144000 | tf_op jit(solution)/shard_map/reshape | solution.py:114
  123.7 15.3 %fusion.14 = bf16[3840,1792]{0,1:T(8,128)(2,1)} fusion(bf16[3840,400]{1,0:T(8,128)(2,1)} %reshape.155, bf16[1792,896]{1,0:T(8,128)(2,1)S(1)} %copy-done, bf16[1792,896]{1,0:T(8,128)(2,1)} %get-tuple-element.155), kind=kOutput, calls=%fused_computation.31 | convolution fusion | flops 5514772480 | bytes 23257088 | tf_op jit(solution)/shard_map/dot_general | solution.py:116
  139.0 18.5 %copy.42 = bf16[3840,1792]{1,0:T(8,128)(2,1)} copy(bf16[3840,1792]{0,1:T(8,128)(2,1)} %fusion.14) | data formatting | bytes 27525120 | tf_op jit(solution)/shard_map/while | solution.py:133
  157.8 20.2 %gather_fusion = s32[3840]{0:T(1024)S(1)} fusion(s32[2448]{0:T(1024)S(1)} %slice.40, s32[4096]{0:T(1024)S(1)} %pad_clamp_fusion.1), kind=kCustom, calls=%fused_computation | custom fusion | bytes 46080 | tf_op jit(solution)/shard_map/jit(_take)/gather | solution.py:119
  178.1 15.8 %negate_convert_fusion = (bf16[896,1024]{1,0:T(8,128)(2,1)S(1)}, bf16[896,1024]{1,0:T(8,128)(2,1)S(1)}) fusion(), kind=kLoop, calls=%fused_computation.51 | loop fusion | flops 11010048 | bytes 3670016 | tf_op jit(solution)/shard_map/convert.3
  196.0 33.3 %gather_fusion.1 = bf16[3840,1792]{1,0:T(8,128)(2,1)} fusion(bf16[4096,1792]{1,0:T(8,128)(2,1)} %all-gather.2.cloned.1.call-done, s32[4096]{0:T(1024)S(1)} %pad_clamp_fusion), kind=kCustom, calls=%fused_computation.1 | custom fusion | bytes 27540480 | tf_op jit(solution)/shard_map/jit(_take)/gather | solution.py:120
  229.4 13.4 %broadcast_select_fusion = bf16[3840,1792]{1,0:T(8,128)(2,1)} fusion(bf16[3840,1792]{1,0:T(8,128)(2,1)} %gather_fusion.1, pred[3840]{0:T(1024)(128)(4,1)S(1)} %compare_and_fusion), kind=kLoop, calls=%fused_computation.30 | loop fusion | flops 6881280 | bytes 27528960 | tf_op jit(solution)/shard_map/jit(_take)/select_n | solution.py:120
  242.8 146.7 %while.12 = (s32[]{:T(128)}, f32[4,32,1024]{2,1,0:T(8,128)}, s32[4]{0:T(128)S(1)}, bf16[3840,1792]{1,0:T(8,128)(2,1)}, bf16[3840,1792]{1,0:T(8,128)(2,1)}, /*ind...) while((s32[]{:T(128)}, f32[4,32,1024]{2,1,0:T(8,128)}, ...), condition=%wide.region_6.7_spmd, body=%wide.region_3.6_spmd.sunk | while | flops 140954240 | bytes 39038152 | solution.py:133
  244.2 20.4 %multiply_subtract_fusion.2 = (f32[960,896]{1,0:T(8,128)}, f32[960,896]{1,0:T(8,128)S(1)}) fusion(s32[960]{0:T(1024)S(1)} %dynamic_slice.28, bf16[3840,1792]{1,0:T(8,128)(2,1)} %get-tuple-element.239, s32[]{:T(128)S(6)} %select_n.188, s32[]{:T(128)S(6)} %add.212, bf16[3840,1792]{1,0:T(8,128)(2,1)} %get-tuple-element.238), kind=kLoop, calls=%fused_computation.12.clone.1 | loop fusion | flops 21504000 | bytes 13766408 | tf_op jit(solution)/shard_map/while/body/eval_jaxpr/sub | solution.py:79
  264.6 4.4 %reshape.183 = f32[32,30,896]{2,1,0:T(8,128)} reshape(f32[960,896]{1,0:T(8,128)} %get-tuple-element.205) | data formatting | bytes 6881280 | tf_op jit(solution)/shard_map/while/body/eval_jaxpr/reshape | solution.py:82
  280.8 20.4 %multiply_subtract_fusion.2 = (f32[960,896]{1,0:T(8,128)}, f32[960,896]{1,0:T(8,128)S(1)}) fusion(s32[960]{0:T(1024)S(1)} %dynamic_slice.28, bf16[3840,1792]{1,0:T(8,128)(2,1)} %get-tuple-element.239, s32[]{:T(128)S(6)} %select_n.188, s32[]{:T(128)S(6)} %add.212, bf16[3840,1792]{1,0:T(8,128)(2,1)} %get-tuple-element.238), kind=kLoop, calls=%fused_computation.12.clone.1 | loop fusion | flops 21504000 | bytes 13766408 | tf_op jit(solution)/shard_map/while/body/eval_jaxpr/sub | solution.py:79
  301.3 4.4 %reshape.183 = f32[32,30,896]{2,1,0:T(8,128)} reshape(f32[960,896]{1,0:T(8,128)} %get-tuple-element.205) | data formatting | bytes 6881280 | tf_op jit(solution)/shard_map/while/body/eval_jaxpr/reshape | solution.py:82
  317.5 20.4 %multiply_subtract_fusion.2 = (f32[960,896]{1,0:T(8,128)}, f32[960,896]{1,0:T(8,128)S(1)}) fusion(s32[960]{0:T(1024)S(1)} %dynamic_slice.28, bf16[3840,1792]{1,0:T(8,128)(2,1)} %get-tuple-element.239, s32[]{:T(128)S(6)} %select_n.188, s32[]{:T(128)S(6)} %add.212, bf16[3840,1792]{1,0:T(8,128)(2,1)} %get-tuple-element.238), kind=kLoop, calls=%fused_computation.12.clone.1 | loop fusion | flops 21504000 | bytes 13766408 | tf_op jit(solution)/shard_map/while/body/eval_jaxpr/sub | solution.py:79
  337.9 4.4 %reshape.183 = f32[32,30,896]{2,1,0:T(8,128)} reshape(f32[960,896]{1,0:T(8,128)} %get-tuple-element.205) | data formatting | bytes 6881280 | tf_op jit(solution)/shard_map/while/body/eval_jaxpr/reshape | solution.py:82
  354.2 20.4 %multiply_subtract_fusion.2 = (f32[960,896]{1,0:T(8,128)}, f32[960,896]{1,0:T(8,128)S(1)}) fusion(s32[960]{0:T(1024)S(1)} %dynamic_slice.28, bf16[3840,1792]{1,0:T(8,128)(2,1)} %get-tuple-element.239, s32[]{:T(128)S(6)} %select_n.188, s32[]{:T(128)S(6)} %add.212, bf16[3840,1792]{1,0:T(8,128)(2,1)} %get-tuple-element.238), kind=kLoop, calls=%fused_computation.12.clone.1 | loop fusion | flops 21504000 | bytes 13766408 | tf_op jit(solution)/shard_map/while/body/eval_jaxpr/sub | solution.py:79
  374.6 4.4 %reshape.183 = f32[32,30,896]{2,1,0:T(8,128)} reshape(f32[960,896]{1,0:T(8,128)} %get-tuple-element.205) | data formatting | bytes 6881280 | tf_op jit(solution)/shard_map/while/body/eval_jaxpr/reshape | solution.py:82
  (113 shorter events, 63.4 us)
Async XLA Ops:
  6.5 12.2 %copy-start.7 = (bf16[64]{0:T(256)(128)(2,1)S(1)}, bf16[64]{0:T(256)(128)(2,1)}, u32[]{:S(2)}) copy-start(bf16[64]{0:T(256)(128)(2,1)} %param.10) | copy-start | bytes 388
  8.9 36.7 %all-to-all-start = ((bf16[16,16,2048]{2,0,1:T(8,128)(2,1)}), bf16[16,16,2048]{2,0,1:T(8,128)(2,1)S(1)}, u32[]{:S(2)}, u32[]{:S(2)}) async-start(bf16[16,16,2048]{2,0,1:T(8,128)(2,1)} %bitcast.25), calls=%async_computation | async-start | bytes 2097152 | tf_op jit(solution)/shard_map/all_to_all | solution.py:97
  18.7 177.3 %all-gather.2.cloned.1.call-start = ((), (), s32[]{:S(2)}) async-start(), calls=%async_computation.1 | async-start | bytes 15597568 | tf_op jit(solution)/shard_map/all_gather | solution.py:109
  46.3 42.4 %collective-permute-start = (bf16[256,1600]{0,1:T(8,128)(2,1)S(1)}, bf16[256,1600]{0,1:T(8,128)(2,1)S(1)}, u32[]{:S(2)}, u32[]{:S(2)}) collective-permute-start(bf16[256,1600]{0,1:T(8,128)(2,1)S(1)} %copy.38), channel_id=1, source_target_pairs={{16,0},{32,16},{48,32},{64,48},{80,64},{96,80},{112,96},{128,112},... | collective-permute-start | bytes 2457608 | tf_op jit(solution)/shard_map/ppermute | solution.py:21
  95.4 1.9 copy-start
  95.4 2.9 copy-start.1
  98.3 4.1 %copy-start.4 = (s32[128,30]{0,1:T(8,128)S(1)}, s32[128,30]{0,1:T(8,128)}, u32[]{:S(2)}) copy-start(s32[128,30]{0,1:T(8,128)} %param.12) | copy-start | bytes 46084
  98.3 4.5 %copy-start.5 = (s32[4096]{0:T(1024)S(1)}, s32[4096]{0:T(1024)}, u32[]{:S(2)}) copy-start(s32[4096]{0:T(1024)} %param.9) | copy-start | bytes 49156
  139.0 18.5 %copy-start.6 = (s32[128,30]{0,1:T(8,128)S(1)}, s32[128,30]{0,1:T(8,128)}, u32[]{:S(2)}) copy-start(s32[128,30]{0,1:T(8,128)} %param.13) | copy-start | bytes 46084
  242.8 21.8 %copy-start.2 = (s32[3840]{0:T(1024)}, s32[3840]{0:T(1024)S(1)}, u32[]{:S(2)}) copy-start(s32[3840]{0:T(1024)S(1)} %get-tuple-element.240) | copy-start | bytes 46084 | tf_op jit(solution)/shard_map/while
  276.0 3.5 copy-start.3
  276.0 3.5 copy-start.9
  279.5 1.4 copy-start.8
  279.5 21.8 %copy-start.2 = (s32[3840]{0:T(1024)}, s32[3840]{0:T(1024)S(1)}, u32[]{:S(2)}) copy-start(s32[3840]{0:T(1024)S(1)} %get-tuple-element.240) | copy-start | bytes 46084 | tf_op jit(solution)/shard_map/while
  312.7 3.5 copy-start.3
  312.7 3.5 copy-start.9
  316.2 1.4 copy-start.8
  316.2 21.8 %copy-start.2 = (s32[3840]{0:T(1024)}, s32[3840]{0:T(1024)S(1)}, u32[]{:S(2)}) copy-start(s32[3840]{0:T(1024)S(1)} %get-tuple-element.240) | copy-start | bytes 46084 | tf_op jit(solution)/shard_map/while
  349.4 3.5 copy-start.3
  349.4 3.5 copy-start.9
  352.8 1.4 copy-start.8
  352.8 21.8 %copy-start.2 = (s32[3840]{0:T(1024)}, s32[3840]{0:T(1024)S(1)}, u32[]{:S(2)}) copy-start(s32[3840]{0:T(1024)S(1)} %get-tuple-element.240) | copy-start | bytes 46084 | tf_op jit(solution)/shard_map/while
  386.0 3.5 copy-start.3
  386.0 3.5 copy-start.9
  (1 other events, 1.4 us)
Sparse Core Ops, SparseCore 0:
  102.5 82.6 all-gather.1
where the time goes:
time: 398 us; the launch traced here: 396 us
  other arithmetic  172 us (43%)
  local copies, waits for them, and re-layouts  127 us (32%)
  waiting for transfers between devices  34.3 us (9%)
  matrix products  34 us (9%)
  between operations  13.6 us (3%)
  starting transfers between devices  12.7 us (3%)
    sub x4, other arithmetic, stack_block(): rotated_real = real_part * phase_cos - imag_part * phase_sin  81.6 us
    another operation x6, other arithmetic  44.2 us
    gather x1, local copies, waits for them, and re-layouts, on_device(): data_all = lax.optimization_barrier(jnp.take(gathered, data_rows, axis=0))  33.3 us
    all_to_all x1, waiting for transfers between devices, on_device(): lax.all_to_all(raw, 'win', split_axis=1, concat_axis=0, tiled=True)  26.8 us
    gather x1, local copies, waits for them, and re-layouts, on_device(): data_rows = jnp.take(row_of, channels.reshape(-1))  20.2 us
    while x1, local copies, waits for them, and re-layouts, on_device(): result = lax.map(one_block, jnp.arange(count, dtype=jnp.int32))  18.5 us
    reshape x4, local copies, waits for them, and re-layouts, stack_block(): summed_real = jnp.sum(rotated_real.reshape(group, CH, NF), axis=1)  17.6 us
    dot_general x1, matrix products, on_device(): jnp.dot(flat_taps, head, preferred_element_type=jnp.float32)  15.3 us
  transfers between devices with their start and end apart: 3, of which 2 were waited for; matrix products, arithmetic and copies ran while one was open for 32% of the time, Pallas kernels for 0%

commit v1 on v0

v1 whole, which is shorter than its diff:
```python
import functools
import math

import jax
import jax.numpy as jnp
import numpy as np
from jax import lax
from jax.experimental import pallas as pl
from jax.experimental.pallas import tpu as pltpu
from jax.sharding import PartitionSpec as P

WIN_DEV = 1024
TL = 400
CH = 30
DEC = 2
NTAP = 64
MOVE = 256
NS = 1792
NF = 896
LANE = 128
FB = NF // LANE
QB = 2 * FB
SLOT = 16
SPAN = DEC * LANE
MIB = 1 << 20


def cos_sin(rows, columns):
    angle = (np.arange(rows)[:, None] * np.arange(columns)[None, :] % NS) * (2.0 * math.pi / NS)
    return np.cos(angle), np.sin(angle)


def forward_table():
    c, s = cos_sin(NS, NF)
    return np.concatenate([c, s], axis=1).astype(jnp.bfloat16)


def inverse_table():
    c, s = cos_sin(NF, WIN_DEV)
    return np.concatenate([c, -s], axis=0).astype(jnp.bfloat16)


def phase_table():
    out = np.zeros((MOVE, 2, 8, LANE), np.float32)
    c, s = cos_sin(MOVE, NF)
    out[:, 0, :FB] = c.reshape(MOVE, FB, LANE)
    out[:, 1, :FB] = s.reshape(MOVE, FB, LANE)
    return out.reshape(MOVE, SLOT, LANE)


def weight_tile():
    w = np.full((NF,), 2.0 / (CH * NS), np.float32)
    w[0] = 1.0 / (CH * NS)
    out = np.zeros((8, LANE), np.float32)
    out[:FB] = w.reshape(FB, LANE)
    return out


def sub(q):
    return q if q < FB else q + 1


def front_kernel(raw_ref, fir_ref, table_ref, out_ref, seg, filt, tile):
    rows = raw_ref.shape[0]
    pieces = raw_ref.shape[1] // SPAN
    wins = out_ref.shape[0] // rows
    per = pieces // wins
    wide = jnp.broadcast_to(fir_ref[...], (LANE, 3 * LANE))
    band = pltpu.roll(wide, 0, 1, stride=DEC, stride_axis=0).astype(jnp.bfloat16)
    for b in range(pieces):
        here = pl.ds(b * rows, rows)
        seg[here, :SPAN] = raw_ref[:, b * SPAN:(b + 1) * SPAN]
        if b + 1 < pieces:
            seg[here, SPAN:] = raw_ref[:, (b + 1) * SPAN:(b + 1) * SPAN + LANE]
        else:
            seg[here, SPAN:] = jnp.zeros((rows, LANE), jnp.bfloat16)
    filt[pl.ds(0, pieces * rows), :] = lax.dot_general(
        seg[...], band, (((1,), (1,)), ((), ())), preferred_element_type=jnp.float32
    ).astype(jnp.bfloat16)
    filt[pl.ds(pieces * rows, FB * rows), :] = jnp.zeros((FB * rows, LANE), jnp.bfloat16)
    for w in range(wins):
        for q in range(QB):
            tile[pl.ds(w * rows, rows), q * LANE:(q + 1) * LANE] = filt[
                pl.ds((w * per + q) * rows, rows), :
            ]
    values = tile[...].astype(jnp.float32)
    scale = lax.rsqrt(jnp.mean(values * values, axis=1, keepdims=True) + 1e-05)
    out_ref[...] = (
        jnp.dot(tile[...], table_ref[...], preferred_element_type=jnp.float32) * scale
    ).astype(jnp.bfloat16)


def front(raw, fir, table, wins):
    rows, length = raw.shape
    pieces = length // SPAN
    wide = jnp.pad(fir.astype(jnp.float32).reshape(1, NTAP), ((0, 0), (0, 3 * LANE - NTAP)))
    return pl.pallas_call(
        front_kernel,
        out_shape=jax.ShapeDtypeStruct((wins * rows, NS), jnp.bfloat16),
        scratch_shapes=[
            pltpu.VMEM((pieces * rows, 3 * LANE), jnp.bfloat16),
            pltpu.VMEM(((pieces + FB) * rows, LANE), jnp.bfloat16),
            pltpu.VMEM((wins * rows, NS), jnp.bfloat16),
        ],
        compiler_params=pltpu.CompilerParams(vmem_limit_bytes=32 * MIB),
        name="front",
    )(raw, wide, table)


TB = 8
CP = 32


def template_kernel(shift_ref, taps_ref, head_ref, phase_ref, out_ref, lhs, spread):
    step = pl.program_id(0)
    for i in range(TB):
        lhs[pl.ds(i * CP, CH), :] = taps_ref[i]
    spec = jnp.dot(lhs[...], head_ref[...], preferred_element_type=jnp.float32)
    for q in range(QB):
        for g in range(TB * CP // 8):
            spread[pl.ds(g * 8 * SLOT + sub(q), 8, stride=SLOT), :] = spec[
                g * 8:(g + 1) * 8, q * LANE:(q + 1) * LANE
            ]

    def one(i, carry):
        for j in range(CH):
            base = pl.multiple_of((i * CP + j) * SLOT, SLOT)
            tc = spread[pl.ds(base, 8), :]
            ts = spread[pl.ds(pl.multiple_of(base + 8, 8), 8), :]
            s = shift_ref[step * TB + i, j]
            pc = phase_ref[s, 0:8, :]
            ps = phase_ref[s, 8:16, :]
            ur = tc * pc - ts * ps
            ui = ts * pc + tc * ps
            out_ref[i * CH + j] = jnp.concatenate([ur, ui], axis=0).astype(jnp.bfloat16)
        return carry

    lax.fori_loop(0, TB, one, 0)


def templates(taps, shifts, head, phase):
    count = taps.shape[0]
    return pl.pallas_call(
        template_kernel,
        out_shape=jax.ShapeDtypeStruct((count * CH, SLOT, LANE), jnp.bfloat16),
        grid_spec=pltpu.PrefetchScalarGridSpec(
            num_scalar_prefetch=1,
            grid=(count // TB,),
            in_specs=[
                pl.BlockSpec((TB, CH, TL), lambda i, s: (i, 0, 0)),
                pl.BlockSpec((TL, NS), lambda i, s: (0, 0)),
                pl.BlockSpec((MOVE, SLOT, LANE), lambda i, s: (0, 0, 0)),
            ],
            out_specs=pl.BlockSpec((TB * CH, SLOT, LANE), lambda i, s: (i, 0, 0)),
            scratch_shapes=[
                pltpu.VMEM((TB * CP, TL), jnp.bfloat16),
                pltpu.VMEM((TB * CP * SLOT, LANE), jnp.float32),
            ],
        ),
        compiler_params=pltpu.CompilerParams(vmem_limit_bytes=32 * MIB),
        cost_estimate=pl.CostEstimate(
            flops=2 * count * CH * TL * NS, bytes_accessed=30 * MIB, transcendentals=0
        ),
        name="templates",
    )(shifts, taps, head, phase)


KB = 8


def stack_kernel(row_ref, chan_ref, u_ref, x_ref, weight_ref, inverse_ref, out_ref, xs, z, packed):
    step = pl.program_id(0)

    @pl.when(step == 0)
    def _():
        def spread(i, carry):
            start = pl.multiple_of(i * 16, 16)
            for q in range(QB):
                v = x_ref[pl.ds(start, 16), q * LANE:(q + 1) * LANE].astype(jnp.float32)
                for h in range(2):
                    xs[pl.ds((start + 8 * h) * SLOT + sub(q), 8, stride=SLOT), :] = v[8 * h:8 * h + 8]
            return carry

        lax.fori_loop(0, x_ref.shape[0] // 16, spread, 0)

    def one(i, carry):
        zr = jnp.zeros((8, LANE), jnp.float32)
        zi = jnp.zeros((8, LANE), jnp.float32)
        for j in range(CH):
            row = row_ref[chan_ref[step * KB + i, j]]
            base = pl.multiple_of(row * SLOT, SLOT)
            xc = xs[pl.ds(base, 8), :]
            xn = xs[pl.ds(pl.multiple_of(base + 8, 8), 8), :]
            u = u_ref[i * CH + j].astype(jnp.float32)
            ur, ui = u[:8], u[8:]
            zr = zr + (ur * xc + ui * xn)
            zi = zi + (ui * xc - ur * xn)
        at = pl.multiple_of((step * KB + i) * SLOT, SLOT)
        z[pl.ds(at, 8), :] = zr * weight_ref[...]
        z[pl.ds(pl.multiple_of(at + 8, 8), 8), :] = zi * weight_ref[...]
        return carry

    lax.fori_loop(0, KB, one, 0)

    @pl.when(step == pl.num_programs(0) - 1)
    def _():
        count = packed.shape[0]
        for q in range(QB):
            for g in range(count // 16):
                halves = [
                    z[pl.ds((g * 16 + 8 * h) * SLOT + sub(q), 8, stride=SLOT), :] for h in range(2)
                ]
                packed[pl.ds(g * 16, 16), q * LANE:(q + 1) * LANE] = jnp.concatenate(
                    halves, axis=0
                ).astype(jnp.bfloat16)
        out_ref[...] = jnp.dot(packed[...], inverse_ref[...], preferred_element_type=jnp.float32)


def stacked(row_of, channels, u, x, weight, inverse):
    count = channels.shape[0]
    held = x.shape[0]
    one = pl.Buffered(1)
    return pl.pallas_call(
        stack_kernel,
        out_shape=jax.ShapeDtypeStruct((count, WIN_DEV), jnp.float32),
        grid_spec=pltpu.PrefetchScalarGridSpec(
            num_scalar_prefetch=2,
            grid=(count // KB,),
            in_specs=[
                pl.BlockSpec((KB * CH, SLOT, LANE), lambda i, r, c: (i, 0, 0)),
                pl.BlockSpec((held, NS), lambda i, r, c: (0, 0), pipeline_mode=one),
                pl.BlockSpec((8, LANE), lambda i, r, c: (0, 0)),
                pl.BlockSpec((NS, WIN_DEV), lambda i, r, c: (0, 0), pipeline_mode=one),
            ],
            out_specs=pl.BlockSpec((count, WIN_DEV), lambda i, r, c: (0, 0)),
            scratch_shapes=[
                pltpu.VMEM((held * SLOT, LANE), jnp.float32),
                pltpu.VMEM((count * SLOT, LANE), jnp.float32),
                pltpu.VMEM((count, NS), jnp.bfloat16),
            ],
        ),
        compiler_params=pltpu.CompilerParams(vmem_limit_bytes=56 * MIB),
        cost_estimate=pl.CostEstimate(
            flops=8 * count * CH * NF, bytes_accessed=30 * MIB, transcendentals=0
        ),
        name="stacked",
    )(row_of, channels, u, x, weight, inverse)


def on_device(raw, ids, fir, taps, channels, shifts):
    wins = lax.axis_size("win")
    tmpls = lax.axis_size("tmpl")
    slots = raw.shape[0]
    live_col = 3 * slots * wins // 5
    chan_total = live_col * tmpls
    held = -(-live_col // 16) * 16

    forward = forward_table()
    spec = front(raw, fir, jnp.asarray(forward), wins)
    mine = lax.all_to_all(
        spec.reshape(wins, slots, NS), "win", split_axis=0, concat_axis=0, tiled=True
    ).reshape(wins * slots, NS)

    grid = ids.reshape(wins, tmpls, slots).transpose(1, 0, 2).reshape(tmpls, wins * slots)
    live = grid >= 0
    rank = jnp.cumsum(live.astype(jnp.int32), axis=1) - 1
    place = jnp.arange(tmpls, dtype=jnp.int32)[:, None] * held + rank
    keyed = jnp.where(live, grid, chan_total)
    _, row_of = lax.sort((keyed.reshape(-1), place.reshape(-1)), num_keys=1)
    row_of = row_of[:chan_total]

    me = lax.axis_index("tmpl")
    my_rank = jnp.where(live, rank, -1)
    my_rank = lax.dynamic_slice_in_dim(my_rank, me, 1, 0)
    pick = (my_rank == jnp.arange(held, dtype=jnp.int32)[:, None]).astype(jnp.bfloat16)
    compact = jnp.dot(pick, mine, preferred_element_type=jnp.float32).astype(jnp.bfloat16)
    x = lax.all_gather(compact, "tmpl", axis=0, tiled=True)

    u = templates(taps, shifts, jnp.asarray(forward[:TL]), jnp.asarray(phase_table()))
    return stacked(
        row_of, channels, u, x, jnp.asarray(weight_tile()), jnp.asarray(inverse_table())
    )


def solution(mesh):
    return jax.shard_map(
        on_device,
        mesh=mesh,
        in_specs=(
            P(("win", "tmpl"), None),
            P(),
            P(),
            P("tmpl", None, None),
            P("tmpl", None),
            P("tmpl", None),
        ),
        out_specs=P("tmpl", "win"),
        check_vma=False,
    )
```

time: 398 us -> 146 us (0.37)
  the two profiles are of different devices: /device:TPU:89 before, /device:TPU:1 now
where the time goes in v1:
time: 146 us; the launch traced here: 145 us
  Pallas kernels  52.9 us (36%)
  waiting for transfers between devices  39.6 us (27%)
  local copies, waits for them, and re-layouts  18.2 us (12%)
  between operations  13.5 us (9%)
  starting transfers between devices  11.9 us (8%)
  other arithmetic  7.38 us (5%)
    pallas_call x1, Pallas kernels, stacked(): pl.pallas_call(stack_kernel, out_shape=jax.ShapeDtypeStruct((count, WIN_D...  27.4 us
    all_to_all x1, waiting for transfers between devices, on_device(): lax.all_to_all(spec.reshape(wins, slots, NS), 'win', split_axis=0, concat...  21.6 us
    pallas_call x1, Pallas kernels, templates(): pl.pallas_call(template_kernel, out_shape=jax.ShapeDtypeStruct((count * C...  21.4 us
    all_gather x1, waiting for transfers between devices, on_device(): x = lax.all_gather(compact, 'tmpl', axis=0, tiled=True)  18 us
    unnamed x23, local copies, waits for them, and re-layouts  16.9 us
    all_to_all x1, starting transfers between devices, on_device(): lax.all_to_all(spec.reshape(wins, slots, NS), 'win', split_axis=0, concat...  11.9 us
    sort x1, other arithmetic, on_device(): _, row_of = lax.sort((keyed.reshape(-1), place.reshape(-1)), num_keys=1)  5.91 us
    pallas_call x1, Pallas kernels, front(): pl.pallas_call(front_kernel, out_shape=jax.ShapeDtypeStruct((wins * rows,...  4.02 us
  transfers between devices with their start and end apart: 2, of which 2 were waited for; matrix products, arithmetic and copies ran while one was open for 12% of the time, Pallas kernels for 15%

profile of v1, /device:TPU:1, one launch (start us, length us, event | category | flops | bytes accessed | tf_op | source)
XLA Modules:
  0.0 144.8 jit_solution(5409011033384120616)
XLA Ops:
  6.5 0.7 pad_convert_fusion.fir_ref
  7.2 2.8 %copy-done.1 = bf16[1792,1792]{1,0:T(8,128)(2,1)S(1)} copy-done((bf16[1792,1792]{1,0:T(8,128)(2,1)S(1)}, bf16[1792,1792]{1,0:T(8,128)(2,1)}, u32[]{:S(2)}) %copy-start.1) | copy-done | bytes 6422552
  10.0 1.2 copy-done.4
  11.2 4.0 %front.1 = bf16[256,1792]{1,0:T(8,128)(2,1)} custom-call(bf16[16,32768]{1,0:T(8,128)(2,1)S(1)} %copy-done.4, f32[1,384]{1,0:T(1,128)S(1)} %pad_convert_fusion.fir_ref, bf16[1792,1792]{1,0:T(8,128)(2,1)S(1)} %copy-done.1), custom_call_target="tpu_custom_call" | custom-call | tf_op jit(solution)/shard_map/front/pallas_call | solution.py:97
  15.3 11.9 %all-to-all-start = ((bf16[16,16,1792]{2,1,0:T(8,128)(2,1)}), bf16[16,16,1792]{2,1,0:T(8,128)(2,1)S(1)}, u32[]{:S(2)}, u32[]{:S(2)}) async-start(bf16[16,16,1792]{2,1,0:T(8,128)(2,1)} %bitcast.4), calls=%async_computation | async-start | bytes 1835008 | tf_op jit(solution)/shard_map/all_to_all | solution.py:260
  27.2 0.1 reshape.48
  27.4 0.1 reshape.54
  27.5 0.6 reduce-window.6
  28.1 0.2 slice_reduce_fusion
  28.4 0.1 ge.20
  28.6 21.6 %all-to-all-done = bf16[16,16,1792]{2,1,0:T(8,128)(2,1)S(1)} async-done(((bf16[16,16,1792]{2,1,0:T(8,128)(2,1)}), bf16[16,16,1792]{2,1,0:T(8,128)(2,1)S(1)}, u32[]{:S(2)}, u32[]{:S(2)}) %all-to-all-start) | async-done | bytes 917536 | tf_op jit(solution)/shard_map/all_to_all | solution.py:260
  50.2 1.2 convolution_convert_fusion
  51.5 0.1 reshape.49
  51.7 0.1 add_add_fusion
  51.8 5.9 %sort.23 = (s32[4096]{0:T(1024)}, s32[4096]{0:T(1024)S(1)}, s32[4096]{0:T(1024)}) sort(s32[4096]{0:T(1024)S(1)} %compare_select_fusion, s32[4096]{0:T(1024)S(1)} %add.22, s32[4096]{0:T(1024)S(1)} %iota.13), dimensions={0}, to_apply=%region_2.3 | sort | flops 49152 | bytes 98304 | tf_op jit(solution)/shard_map/sort | solution.py:269
  57.7 0.6 slice.11.row_ref
  58.3 0.7 copy.29.chan_ref
  59.1 0.7 copy.25.shift_ref
  59.8 8.2 %copy.26.taps_ref = bf16[128,30,400]{2,1,0:T(8,128)(2,1)} copy(bf16[128,30,400]{0,2,1:T(8,128)(2,1)} %param.14) | data formatting | bytes 6144000 | tf_op args[3]
  68.0 2.3 %copy-done = bf16[128,30,400]{2,1,0:T(8,128)(2,1)S(1)} copy-done((bf16[128,30,400]{2,1,0:T(8,128)(2,1)S(1)}, bf16[128,30,400]{2,1,0:T(8,128)(2,1)}, u32[]{:S(2)}) %copy-start) | copy-done | bytes 3072024
  70.2 0.8 copy-done.5
  71.1 21.4 %templates.1.u_ref = bf16[3840,16,128]{2,1,0:T(8,128)(2,1)} custom-call(s32[128,30]{1,0:T(8,128)S(1)} %copy-done.5, bf16[128,30,400]{2,1,0:T(8,128)(2,1)S(1)} %copy-done, bf16[400,1792]{1,0:T(8,128)(2,1)S(1)} %copy-done.3, f32[256,16,128]{2,1,0:T(8,128)S(1)} %copy-done.2), custom_call_target="tpu_custom_call" | custom-call | flops 5505024000 | bytes 31457280 | tf_op jit(solution)/shard_map/templates/pallas_call | solution.py:143
  92.5 18.0 %all-gather.2.cloned.1.call-done.x_ref = bf16[2560,1792]{1,0:T(8,128)(2,1)} async-done(((bf16[160,1792]{1,0:T(8,128)(2,1)}), bf16[2560,1792]{1,0:T(8,128)(2,1)}) %all-gather.2.cloned.1.call-update) | async-done | bytes 9175056 | tf_op jit(solution)/shard_map/all_gather | solution.py:277
  110.5 27.4 %stacked.1 = f32[128,1024]{1,0:T(8,128)} custom-call(s32[2448]{0:T(1024)} %slice.11.row_ref, s32[128,30]{1,0:T(8,128)} %copy.29.chan_ref, bf16[3840,16,128]{2,1,0:T(8,128)(2,1)} %templates.1.u_ref, bf16[2560,1792]{1,0:T(8,128)(2,1)} %all-gather.2.cloned.1.call-done.x_ref, f32[8,128]{1,0:T(8,128)} %constant.36.clone.weight_ref, ...), custom_call_target="tpu_custom_call" | custom-call | flops 27525120 | bytes 31457280 | tf_op jit(solution)/shard_map/stacked/pallas_call | solution.py:223
  (32 shorter events, 0.5 us)
Async XLA Ops:
  7.2 2.8 %copy-start.1 = (bf16[1792,1792]{1,0:T(8,128)(2,1)S(1)}, bf16[1792,1792]{1,0:T(8,128)(2,1)}, u32[]{:S(2)}) copy-start(bf16[1792,1792]{1,0:T(8,128)(2,1)} %constant.33.clone.table_ref) | copy-start | bytes 19267588
  10.0 1.2 copy-start.4
  11.2 16.0 %copy-start.6 = (s32[4096]{0:T(1024)S(1)}, s32[4096]{0:T(1024)}, u32[]{:S(2)}) copy-start(s32[4096]{0:T(1024)} %param.12) | copy-start | bytes 49156
  15.3 43.1 %copy-start.7 = (s32[128,30]{0,1:T(8,128)S(1)}, s32[128,30]{0,1:T(8,128)}, u32[]{:S(2)}) copy-start(s32[128,30]{0,1:T(8,128)} %param.15) | copy-start | bytes 46084
  15.3 43.8 %copy-start.8 = (s32[128,30]{0,1:T(8,128)S(1)}, s32[128,30]{0,1:T(8,128)}, u32[]{:S(2)}) copy-start(s32[128,30]{0,1:T(8,128)} %param.16) | copy-start | bytes 46084
  15.3 35.0 %all-to-all-start = ((bf16[16,16,1792]{2,1,0:T(8,128)(2,1)}), bf16[16,16,1792]{2,1,0:T(8,128)(2,1)S(1)}, u32[]{:S(2)}, u32[]{:S(2)}) async-start(bf16[16,16,1792]{2,1,0:T(8,128)(2,1)} %bitcast.4), calls=%async_computation | async-start | bytes 1835008 | tf_op jit(solution)/shard_map/all_to_all | solution.py:260
  27.2 83.3 %all-gather.2.cloned.1.call-start = ((), (), s32[]{:S(2)}) async-start(), calls=%async_computation.1 | async-start | bytes 9748480 | tf_op jit(solution)/shard_map/all_gather | solution.py:277
  59.1 8.9 %copy-start.2 = (f32[256,16,128]{2,1,0:T(8,128)S(1)}, f32[256,16,128]{2,1,0:T(8,128)}, u32[]{:S(2)}) copy-start(f32[256,16,128]{2,1,0:T(8,128)} %constant.35.clone.phase_ref) | copy-start | bytes 6291460
  59.1 8.9 %copy-start.3 = (bf16[400,1792]{1,0:T(8,128)(2,1)S(1)}, bf16[400,1792]{1,0:T(8,128)(2,1)}, u32[]{:S(2)}) copy-start(bf16[400,1792]{1,0:T(8,128)(2,1)} %constant.34.clone.head_ref) | copy-start | bytes 4300804
  68.0 2.3 %copy-start = (bf16[128,30,400]{2,1,0:T(8,128)(2,1)S(1)}, bf16[128,30,400]{2,1,0:T(8,128)(2,1)}, u32[]{:S(2)}) copy-start(bf16[128,30,400]{2,1,0:T(8,128)(2,1)} %copy.26.taps_ref) | copy-start | bytes 9216004
  70.2 0.8 copy-start.5
Sparse Core Ops, SparseCore 0:
  51.6 58.8 all-gather.1

commit v2 on v1

v2 whole, which is shorter than its diff:
```python
import functools
import math

import jax
import jax.numpy as jnp
import numpy as np
from jax import lax
from jax.experimental import pallas as pl
from jax.experimental.pallas import tpu as pltpu
from jax.sharding import PartitionSpec as P

WIN_DEV = 1024
TL = 400
CH = 30
DEC = 2
NTAP = 64
MOVE = 256
NS = 1792
NF = 896
LANE = 128
FB = NF // LANE
QB = 2 * FB
SLOT = 16
SPAN = DEC * LANE
SLOTS = 16
TMPL = 16
MIB = 1 << 20


def cos_sin(rows, columns):
    angle = (np.arange(rows)[:, None] * np.arange(columns)[None, :] % NS) * (2.0 * math.pi / NS)
    return np.cos(angle), np.sin(angle)


def forward_table():
    c, s = cos_sin(NS, NF)
    return np.concatenate([c, s], axis=1).astype(jnp.bfloat16)


def inverse_table():
    c, s = cos_sin(NF, WIN_DEV)
    return np.concatenate([c, -s], axis=0).astype(jnp.bfloat16)


def phase_table():
    out = np.zeros((MOVE, 2, 8, LANE), np.float32)
    c, s = cos_sin(MOVE, NF)
    out[:, 0, :FB] = c.reshape(MOVE, FB, LANE)
    out[:, 1, :FB] = s.reshape(MOVE, FB, LANE)
    return out.reshape(MOVE, SLOT, LANE)


def weight_tile():
    w = np.full((NF,), 2.0 / (CH * NS), np.float32)
    w[0] = 1.0 / (CH * NS)
    out = np.zeros((8, LANE), np.float32)
    out[:FB] = w.reshape(FB, LANE)
    return out


def sub(q):
    return q if q < FB else q + 1


def dot(a, b, dims=((1,), (0,))):
    return lax.dot_general(a, b, (dims, ((), ())), preferred_element_type=jnp.float32)


def plan(ids_ref, rows_ref, rank_ref, held):
    ids = ids_ref[...]
    count, lanes = ids.shape
    group = lanes // SLOTS
    per = TMPL // group
    live = ids >= 0
    livef = live.astype(jnp.float32).astype(jnp.bfloat16)
    la = lax.broadcasted_iota(jnp.int32, (lanes, lanes), 0)
    lb = lax.broadcasted_iota(jnp.int32, (lanes, lanes), 1)
    same = (la // SLOTS) == (lb // SLOTS)
    total = dot(livef, same.astype(jnp.float32).astype(jnp.bfloat16)).astype(jnp.bfloat16)
    upto = dot(livef, (same & (la <= lb)).astype(jnp.float32).astype(jnp.bfloat16))
    ra = lax.broadcasted_iota(jnp.int32, (count, count), 0)
    rb = lax.broadcasted_iota(jnp.int32, (count, count), 1)
    before = ((ra % per) == (rb % per)) & (rb < ra)
    rank = upto + dot(before.astype(jnp.float32).astype(jnp.bfloat16), total)
    rank = jnp.where(live, rank, 0.0)
    row = lax.broadcasted_iota(jnp.int32, (count, lanes), 0)
    lane = lax.broadcasted_iota(jnp.int32, (count, lanes), 1)
    column = (row % per) * group + lane // SLOTS
    place = column * held + rank.astype(jnp.int32) - 1

    slots = count // per * SLOTS
    me = lax.axis_index("tmpl")
    sa = lax.broadcasted_iota(jnp.int32, (lanes, slots), 0)
    sb = lax.broadcasted_iota(jnp.int32, (lanes, slots), 1)
    chosen = sa == (me % group) * SLOTS + (sb % SLOTS)
    mine = dot(rank.astype(jnp.bfloat16), chosen.astype(jnp.float32).astype(jnp.bfloat16))
    oa = lax.broadcasted_iota(jnp.int32, (count, slots), 0)
    ob = lax.broadcasted_iota(jnp.int32, (count, slots), 1)
    mine = jnp.where(oa == (ob // SLOTS) * per + me // group, mine, 0.0)
    rank_ref[...] = jnp.broadcast_to(jnp.sum(mine, axis=0, keepdims=True), rank_ref.shape)

    high = rows_ref.shape[0]
    hi_iota = lax.broadcasted_iota(jnp.int32, (high, lanes), 0)
    lo_iota = lax.broadcasted_iota(jnp.int32, (LANE, lanes), 0)
    hi_sum = jnp.zeros((high, LANE), jnp.float32)
    lo_sum = jnp.zeros((high, LANE), jnp.float32)
    for r in range(count):
        label = ids[r:r + 1]
        at = place[r:r + 1]
        hit = hi_iota == (label >> 7)
        hi = jnp.where(hit, (at >> 6).astype(jnp.float32), 0.0).astype(jnp.bfloat16)
        lo = jnp.where(hit, (at & 63).astype(jnp.float32), 0.0).astype(jnp.bfloat16)
        low = (lo_iota == (label & 127)).astype(jnp.float32).astype(jnp.bfloat16)
        hi_sum = hi_sum + dot(hi, low, ((1,), (1,)))
        lo_sum = lo_sum + dot(lo, low, ((1,), (1,)))
    rows_ref[...] = hi_sum.astype(jnp.int32) * 64 + lo_sum.astype(jnp.int32)


def front_kernel(held, raw_ref, fir_ref, ids_ref, table_hbm, out_ref, rows_ref, rank_ref, seg, filt, tile, table, sem):
    fetch = pltpu.make_async_copy(table_hbm, table, sem)
    fetch.start()
    rows = raw_ref.shape[0]
    pieces = raw_ref.shape[1] // SPAN
    wins = out_ref.shape[0] // rows
    per = pieces // wins
    wide = jnp.broadcast_to(fir_ref[...], (LANE, 3 * LANE))
    band = pltpu.roll(wide, 0, 1, stride=DEC, stride_axis=0).astype(jnp.bfloat16)
    for b in range(pieces):
        here = pl.ds(b * rows, rows)
        seg[here, :SPAN] = raw_ref[:, b * SPAN:(b + 1) * SPAN]
        if b + 1 < pieces:
            seg[here, SPAN:] = raw_ref[:, (b + 1) * SPAN:(b + 1) * SPAN + LANE]
        else:
            seg[here, SPAN:] = jnp.zeros((rows, LANE), jnp.bfloat16)
    filt[pl.ds(0, pieces * rows), :] = dot(seg[...], band, ((1,), (1,))).astype(jnp.bfloat16)
    filt[pl.ds(pieces * rows, FB * rows), :] = jnp.zeros((FB * rows, LANE), jnp.bfloat16)
    for w in range(wins):
        for q in range(QB):
            tile[pl.ds(w * rows, rows), q * LANE:(q + 1) * LANE] = filt[
                pl.ds((w * per + q) * rows, rows), :
            ]
    plan(ids_ref, rows_ref, rank_ref, held)
    values = tile[...].astype(jnp.float32)
    scale = lax.rsqrt(jnp.mean(values * values, axis=1, keepdims=True) + 1e-05)
    fetch.wait()
    out_ref[...] = (dot(tile[...], table[...]) * scale).astype(jnp.bfloat16)


def front(raw, fir, ids, table, wins, held, high):
    rows, length = raw.shape
    pieces = length // SPAN
    wide = jnp.pad(fir.astype(jnp.float32).reshape(1, NTAP), ((0, 0), (0, 3 * LANE - NTAP)))
    vmem = pl.BlockSpec(memory_space=pltpu.VMEM)
    return pl.pallas_call(
        functools.partial(front_kernel, held),
        out_shape=(
            jax.ShapeDtypeStruct((wins * rows, NS), jnp.bfloat16),
            jax.ShapeDtypeStruct((high, LANE), jnp.int32),
            jax.ShapeDtypeStruct((8, wins * rows), jnp.float32),
        ),
        in_specs=[vmem, vmem, vmem, pl.BlockSpec(memory_space=pl.ANY)],
        out_specs=(vmem, vmem, vmem),
        scratch_shapes=[
            pltpu.VMEM((pieces * rows, 3 * LANE), jnp.bfloat16),
            pltpu.VMEM(((pieces + FB) * rows, LANE), jnp.bfloat16),
            pltpu.VMEM((wins * rows, NS), jnp.bfloat16),
            pltpu.VMEM((NS, NS), jnp.bfloat16),
            pltpu.SemaphoreType.DMA,
        ],
        compiler_params=pltpu.CompilerParams(vmem_limit_bytes=32 * MIB),
        name="front",
    )(raw, wide, ids, table)


JB = 2
UNROLL = 32


def template_spectra(shift_ref, taps, head, phase, u, spread):
    count = taps.shape[2]
    steps = taps.shape[0] // JB
    many = JB * count
    turns = count // UNROLL

    def one(step, carry):
        lhs = jnp.concatenate([taps[step * JB + j].T for j in range(JB)], axis=0)
        for c in range(NS // SPAN):
            spec = dot(lhs, head[:, c * SPAN:(c + 1) * SPAN])
            for h in range(2):
                for g in range(many // 8):
                    spread[pl.ds((g * QB + 2 * c + h) * 8, 8), :] = spec[
                        g * 8:(g + 1) * 8, h * LANE:(h + 1) * LANE
                    ]

        def rows(i, inner):
            for r in range(UNROLL):
                row = i * UNROLL + r
                base = i * (UNROLL // 8 * QB * 8) + (r // 8) * QB * 8 + r % 8
                tc = spread[pl.ds(base, 8, stride=8), :]
                ts = spread[pl.ds(base + FB * 8, 8, stride=8), :]
                s = shift_ref[step * JB + i // turns, (i % turns) * UNROLL + r]
                pc = phase[s, 0:8, :]
                ps = phase[s, 8:16, :]
                u[step * many + row] = jnp.concatenate(
                    [tc * pc - ts * ps, ts * pc + tc * ps], axis=0
                ).astype(jnp.bfloat16)
            return inner

        lax.fori_loop(0, many // UNROLL, rows, 0)
        return carry

    lax.fori_loop(0, steps, one, 0)


MESH = pl.DeviceIdType.MESH


def exchange_kernel(
    wins, rows_ref, chan_ref, shift_ref, spec_ref, rank_ref, weight_ref,
    taps_hbm, head_hbm, phase_hbm, inverse_hbm,
    out_ref,
    mine, wide, buf, u, spread, z, packed, taps, head, phase, inverse,
    fetch_sem, a_send, a_recv, g_send, g_recv,
):
    slots = spec_ref.shape[0] // wins
    w = lax.axis_index("win")
    t = lax.axis_index("tmpl")
    held = buf.shape[1]
    zl, x, c = t // 8, (t // 2) % 4, t % 2

    def ix(a, b, d):
        return (a * 4 + b) * 2 + d

    zo, xp, xm, x2, co = 1 - zl, lax.rem(x + 1, 4), lax.rem(x + 3, 4), lax.rem(x + 2, 4), 1 - c
    up, down, over, beside, me = ix(zl, xp, c), ix(zl, xm, c), ix(zo, x, c), ix(zl, x, co), ix(zl, x, c)

    barrier = pltpu.get_barrier_semaphore()
    for d in range(1, wins):
        pl.semaphore_signal(
            barrier, inc=1, device_id={"win": lax.rem(w + d, wins)}, device_id_type=MESH
        )
    for d in (up, down, over, beside):
        pl.semaphore_signal(barrier, inc=1, device_id={"tmpl": d}, device_id_type=MESH)

    fetches = [
        pltpu.make_async_copy(a, b, fetch_sem.at[i])
        for i, (a, b) in enumerate(
            ((taps_hbm, taps), (head_hbm, head), (phase_hbm, phase), (inverse_hbm, inverse))
        )
    ]
    for f in fetches:
        f.start()
    pl.semaphore_wait(barrier, wins + 3)

    def block(ref, i):
        return ref.at[pl.ds(pl.multiple_of(i * slots, slots), slots)]

    moves = []
    for d in range(1, wins):
        to = lax.rem(w + d, wins)
        move = pltpu.make_async_remote_copy(
            src_ref=block(spec_ref, to), dst_ref=block(mine, w),
            send_sem=a_send.at[d - 1], recv_sem=a_recv.at[d - 1],
            device_id={"win": to}, device_id_type=MESH,
        )
        move.start()
        moves.append(move)
    own = pl.ds(pl.multiple_of(w * slots, slots), slots)
    mine[own, :] = spec_ref[own, :]

    for f in fetches:
        f.wait()
    template_spectra(shift_ref, taps, head, phase, u, spread)

    for move in moves:
        move.wait_recv()
    tall = wide.shape[0] // SLOT
    order = lax.broadcasted_iota(jnp.int32, (tall, mine.shape[0]), 0).astype(jnp.float32) + 1.0
    pick = (order == rank_ref[0:1, :]).astype(jnp.float32).astype(jnp.bfloat16)
    for b in range(NS // SPAN):
        part = dot(pick, mine[:, b * SPAN:(b + 1) * SPAN])
        for h in range(2):
            for g in range(tall // 8):
                wide[pl.ds(g * 8 * SLOT + sub(2 * b + h), 8, stride=SLOT), :] = part[
                    g * 8:(g + 1) * 8, h * LANE:(h + 1) * LANE
                ]
    for g in range(held):
        buf[me, g] = wide[pl.ds(g * SLOT, SLOT), :].astype(jnp.bfloat16)

    cut = held * 2 // 5
    rest = held - cut
    low, high, whole = (0, cut), (cut, rest), (0, held)
    low1, low2 = (0, cut // 2), (cut // 2, cut - cut // 2)
    high1, high2 = (cut, rest // 2), (cut + rest // 2, rest - rest // 2)
    sends, beside_recv = [], []

    def copy(of, seg, to, k):
        ref = buf.at[of, pl.ds(seg[0], seg[1])]
        return pltpu.make_async_remote_copy(
            src_ref=ref, dst_ref=ref, send_sem=g_send.at[k], recv_sem=g_recv.at[k],
            device_id={"tmpl": to}, device_id_type=MESH,
        )

    def send(of, seg, to, back):
        k = len(sends)
        s = copy(of, seg, to, k)
        s.start()
        sends.append(s)
        return copy(back, seg, to, k)

    def relay(a, b, seg):
        beside_recv.append(send(ix(a, b, c), seg, beside, ix(a, b, co)))

    z_high = send(me, high, over, ix(zo, x, c))
    up_low = send(me, low, up, ix(zl, xm, c))
    down_low = send(me, low, down, ix(zl, xp, c))
    up_high = send(me, high, up, ix(zl, xm, c))
    down_high = send(me, high, down, ix(zl, xp, c))
    z_low = send(me, low, over, ix(zo, x, c))
    relay(zl, x, whole)
    up_low.wait_recv()
    up_low1 = send(ix(zl, xm, c), low1, up, ix(zl, x2, c))
    z_low_m = send(ix(zl, xm, c), low, over, ix(zo, xm, c))
    relay(zl, xm, low)
    down_low.wait_recv()
    down_low2 = send(ix(zl, xp, c), low2, down, ix(zl, x2, c))
    z_low_p = send(ix(zl, xp, c), low, over, ix(zo, xp, c))
    relay(zl, xp, low)
    z_high.wait_recv()
    up_z = send(ix(zo, x, c), high, up, ix(zo, xm, c))
    down_z = send(ix(zo, x, c), high, down, ix(zo, xp, c))
    relay(zo, x, high)
    up_high.wait_recv()
    up_high1 = send(ix(zl, xm, c), high1, up, ix(zl, x2, c))
    relay(zl, xm, high)
    down_high.wait_recv()
    down_high2 = send(ix(zl, xp, c), high2, down, ix(zl, x2, c))
    relay(zl, xp, high)
    z_low.wait_recv()
    relay(zo, x, low)
    up_low1.wait_recv()
    z_low1 = send(ix(zl, x2, c), low1, over, ix(zo, x2, c))
    relay(zl, x2, low1)
    down_low2.wait_recv()
    z_low2 = send(ix(zl, x2, c), low2, over, ix(zo, x2, c))
    relay(zl, x2, low2)
    up_z.wait_recv()
    up_z1 = send(ix(zo, xm, c), high1, up, ix(zo, x2, c))
    relay(zo, xm, high)
    down_z.wait_recv()
    down_z2 = send(ix(zo, xp, c), high2, down, ix(zo, x2, c))
    relay(zo, xp, high)
    z_low_m.wait_recv()
    relay(zo, xm, low)
    z_low_p.wait_recv()
    relay(zo, xp, low)
    up_high1.wait_recv()
    relay(zl, x2, high1)
    down_high2.wait_recv()
    relay(zl, x2, high2)
    z_low1.wait_recv()
    relay(zo, x2, low1)
    z_low2.wait_recv()
    relay(zo, x2, low2)
    up_z1.wait_recv()
    relay(zo, x2, high1)
    down_z2.wait_recv()
    relay(zo, x2, high2)
    for r in beside_recv:
        r.wait_recv()

    count = chan_ref.shape[1]
    flat = buf.reshape(buf.shape[0] * held, SLOT, LANE)

    def template(k):
        zr = [jnp.zeros((8, LANE), jnp.float32)] * 2
        zi = [jnp.zeros((8, LANE), jnp.float32)] * 2
        for j in range(CH):
            name = chan_ref[j, k]
            xv = flat[rows_ref[name >> 7, name & 127]].astype(jnp.float32)
            uv = u[j * count + k].astype(jnp.float32)
            xc, xs, ur, ui = xv[:8], xv[8:], uv[:8], uv[8:]
            a = j % 2
            zr[a] = zr[a] + (ur * xc + ui * xs)
            zi[a] = zi[a] + (ui * xc - ur * xs)
        at = pl.multiple_of(k * SLOT, SLOT)
        z[pl.ds(at, 8), :] = (zr[0] + zr[1]) * weight_ref[...]
        z[pl.ds(pl.multiple_of(at + 8, 8), 8), :] = (zi[0] + zi[1]) * weight_ref[...]

    def two(i, carry):
        template(2 * i)
        template(2 * i + 1)
        return carry

    lax.fori_loop(0, count // 2, two, 0)
    for q in range(QB):
        for g in range(count // 16):
            halves = [
                z[pl.ds((g * 16 + 8 * h) * SLOT + sub(q), 8, stride=SLOT), :] for h in range(2)
            ]
            packed[pl.ds(g * 16, 16), q * LANE:(q + 1) * LANE] = jnp.concatenate(
                halves, axis=0
            ).astype(jnp.bfloat16)
    out_ref[...] = dot(packed[...], inverse[...])

    for move in moves:
        move.wait_send()
    for s in sends:
        s.wait_send()


def exchange(rows, channels, shifts, spec, rank, taps, wins, tmpls, held):
    count = taps.shape[2]
    consts = (
        jnp.asarray(forward_table()[:TL]), jnp.asarray(phase_table()), jnp.asarray(inverse_table())
    )
    smem = pl.BlockSpec(memory_space=pltpu.SMEM)
    vmem = pl.BlockSpec(memory_space=pltpu.VMEM)
    hbm = pl.BlockSpec(memory_space=pl.ANY)
    tall = -(-held // 16) * 16
    return pl.pallas_call(
        functools.partial(exchange_kernel, wins),
        out_shape=jax.ShapeDtypeStruct((count, WIN_DEV), jnp.float32),
        in_specs=[smem, smem, smem, vmem, vmem, vmem, hbm, hbm, hbm, hbm],
        out_specs=vmem,
        scratch_shapes=[
            pltpu.VMEM(spec.shape, jnp.bfloat16),
            pltpu.VMEM((tall * SLOT, LANE), jnp.float32),
            pltpu.VMEM((tmpls, held, SLOT, LANE), jnp.bfloat16),
            pltpu.VMEM((count * CH, SLOT, LANE), jnp.bfloat16),
            pltpu.VMEM((JB * count * SLOT, LANE), jnp.float32),
            pltpu.VMEM((count * SLOT, LANE), jnp.float32),
            pltpu.VMEM((count, NS), jnp.bfloat16),
            pltpu.VMEM(taps.shape, jnp.bfloat16),
            pltpu.VMEM((TL, NS), jnp.bfloat16),
            pltpu.VMEM((MOVE, SLOT, LANE), jnp.float32),
            pltpu.VMEM((NS, WIN_DEV), jnp.bfloat16),
            pltpu.SemaphoreType.DMA((4,)),
            pltpu.SemaphoreType.DMA((wins - 1,)),
            pltpu.SemaphoreType.DMA((wins - 1,)),
            pltpu.SemaphoreType.DMA((37,)),
            pltpu.SemaphoreType.DMA((37,)),
        ],
        compiler_params=pltpu.CompilerParams(
            vmem_limit_bytes=58 * MIB, collective_id=0, has_side_effects=True
        ),
        name="exchange",
    )(rows, channels, shifts, spec, rank, jnp.asarray(weight_tile()), taps, *consts)


def on_device(raw, ids, fir, taps, channels, shifts):
    wins = lax.axis_size("win")
    tmpls = lax.axis_size("tmpl")
    held = 3 * SLOTS * wins // 5
    high = -(-held * tmpls // (8 * LANE)) * 8
    spec, rows, rank = front(
        raw, fir, ids.reshape(-1, LANE), jnp.asarray(forward_table()), wins, held, high
    )
    return exchange(
        rows, channels.T, shifts.T, spec, rank, jnp.transpose(taps, (1, 2, 0)), wins, tmpls, held
    )


def solution(mesh):
    return jax.shard_map(
        on_device,
        mesh=mesh,
        in_specs=(
            P(("win", "tmpl"), None),
            P(),
            P(),
            P("tmpl", None, None),
            P("tmpl", None),
            P("tmpl", None),
        ),
        out_specs=P("tmpl", "win"),
        check_vma=False,
    )
```

time: 146 us -> 105 us (0.72)
  Pallas kernels: 52.9 us -> 95 us
  waiting for transfers between devices: 39.6 us -> 0 us
  between operations: 13.5 us -> 0.03 us
  starting transfers between devices: 11.9 us -> 0 us
  local copies, waits for them, and re-layouts: 18.2 us -> 8.78 us
  other arithmetic: 7.38 us -> 0.66 us
    pallas_call x3 -> x2, Pallas kernels: 52.9 us -> 95 us  [the longest x1 88.2 us: exchange(): pl.pallas_call(functools.partial(exchange_kernel, wins), out_shape=jax.Sh...]
    all_to_all x1 -> x0, waiting for transfers between devices: 21.6 us -> none  [on_device(): lax.all_to_all(spec.reshape(wins, slots, NS), 'win', split_axis=0, concat...]
    all_gather x1 -> x0, waiting for transfers between devices: 18 us -> none  [on_device(): x = lax.all_gather(compact, 'tmpl', axis=0, tiled=True)]
    all_to_all x1 -> x0, starting transfers between devices: 11.9 us -> none  [on_device(): lax.all_to_all(spec.reshape(wins, slots, NS), 'win', split_axis=0, concat...]
    unnamed x23 -> x13, local copies, waits for them, and re-layouts: 16.9 us -> 8.78 us
    sort x1 -> x0, other arithmetic: 5.91 us -> none  [on_device(): _, row_of = lax.sort((keyed.reshape(-1), place.reshape(-1)), num_keys=1)]
  transfers between devices with their start and end apart: 2 -> 0, of which waited for: 2 -> 0; matrix products, arithmetic and copies ran while one was open for 12% -> 0% of each run, Pallas kernels for 15% -> 0%
where the time goes in v2:
time: 105 us; the launch traced here: 104 us
  Pallas kernels  95 us (90%)
  local copies, waits for them, and re-layouts  8.78 us (8%)
    pallas_call x1, Pallas kernels, exchange(): pl.pallas_call(functools.partial(exchange_kernel, wins), out_shape=jax.Sh...  88.2 us
    unnamed x13, local copies, waits for them, and re-layouts  8.78 us
    pallas_call x1, Pallas kernels, front(): pl.pallas_call(functools.partial(front_kernel, held), out_shape=(jax.Shap...  6.85 us

profile of v2, /device:TPU:1, one launch (start us, length us, event | category | flops | bytes accessed | tf_op | source)
XLA Modules:
  0.0 104.5 jit_solution(12124991718289239824)
XLA Ops:
  0.0 0.7 pad_convert_fusion.fir_ref
  0.7 0.0 copy-start
  0.7 2.8 %copy-done = bf16[1792,1792]{1,0:T(8,128)(2,1)S(1)} copy-done((bf16[1792,1792]{1,0:T(8,128)(2,1)S(1)}, bf16[1792,1792]{1,0:T(8,128)(2,1)}, u32[]{:S(2)}) %copy-start) | copy-done | bytes 6422552
  3.5 0.0 copy-start.1
  3.5 1.2 %copy-done.1 = bf16[16,32768]{1,0:T(8,128)(2,1)S(1)} copy-done((bf16[16,32768]{1,0:T(8,128)(2,1)S(1)}, bf16[16,32768]{1,0:T(8,128)(2,1)}, u32[]{:S(2)}) %copy-start.1) | copy-done | bytes 1048600
  4.7 0.0 copy-start.3
  4.7 0.7 copy-done.3
  5.4 6.8 %front.1 = (bf16[256,1792]{1,0:T(8,128)(2,1)S(1)}, s32[24,128]{1,0:T(8,128)S(1)}, f32[8,256]{1,0:T(8,128)S(1)}) custom-call(bf16[16,32768]{1,0:T(8,128)(2,1)S(1)} %copy-done.1, f32[1,384]{1,0:T(1,128)S(1)} %pad_convert_fusion.fir_ref, s32[32,128]{1,0:T(8,128)S(1)} %bitcast.5, bf16[1792,1792]{1,0:T(8,128)(2,1)S(1)} %copy-done), custom_call_target="tpu_custom_call" | custom-call | tf_op jit(solution)/shard_map/front/pallas_call | solution.py:154
  12.3 0.0 copy-start.2
  12.3 0.9 copy-done.2
  13.2 0.0 copy-start.4
  13.2 0.6 copy-done.4
  13.8 0.0 copy-start.5
  13.8 0.6 copy-done.5
  14.4 88.2 %exchange.1 = f32[128,1024]{1,0:T(8,128)} custom-call(s32[24,128]{1,0:T(8,128)} %copy-done.4, s32[30,128]{1,0:T(8,128)} %bitcast.7, s32[30,128]{1,0:T(8,128)} %bitcast.8, bf16[256,1792]{1,0:T(8,128)(2,1)} %copy-done.2, f32[8,256]{1,0:T(8,128)} %copy-done.5, f32[8,128]{1,0:T(8,128)} %constant.18.clone.weight_ref, bf16[30,400,128]{2,1,0:T(8,128)(2,1)} %bitcast.6, ...), custom_call_target="tpu_custom_call" | custom-call | tf_op jit(solution)/shard_map/exchange/pallas_call | solution.py:421
  102.6 1.9 %copy.13 = f32[128,1024]{1,0:T(8,128)} copy(f32[128,1024]{1,0:T(8,128)} %exchange.1) | data formatting | bytes 1048576
Async XLA Ops:
  0.7 2.8 %copy-start = (bf16[1792,1792]{1,0:T(8,128)(2,1)S(1)}, bf16[1792,1792]{1,0:T(8,128)(2,1)}, u32[]{:S(2)}) copy-start(bf16[1792,1792]{1,0:T(8,128)(2,1)} %constant.14.clone.table_hbm) | copy-start | bytes 19267588
  3.5 1.2 %copy-start.1 = (bf16[16,32768]{1,0:T(8,128)(2,1)S(1)}, bf16[16,32768]{1,0:T(8,128)(2,1)}, u32[]{:S(2)}) copy-start(bf16[16,32768]{1,0:T(8,128)(2,1)} %raw_ref.1) | copy-start | bytes 3145732
  4.7 0.7 copy-start.3
  12.3 1.0 copy-start.2
  13.2 0.6 copy-start.4
  13.8 0.6 copy-start.5

commit v3 on v2

v3 whole, which is shorter than its diff:
```python
import functools
import math

import jax
import jax.numpy as jnp
import numpy as np
from jax import lax
from jax.experimental import pallas as pl
from jax.experimental.pallas import tpu as pltpu
from jax.sharding import PartitionSpec as P

WIN_DEV = 1024
TL = 400
CH = 30
DEC = 2
NTAP = 64
MOVE = 256
NS = 1792
NF = 896
LANE = 128
FB = NF // LANE
QB = 2 * FB
SLOT = 16
SPAN = DEC * LANE
SLOTS = 16
TMPL = 16
CUT_C = 0
CUT_S = 61
MIB = 1 << 20


def cos_sin(rows, columns):
    angle = (np.arange(rows)[:, None] * np.arange(columns)[None, :] % NS) * (2.0 * math.pi / NS)
    return np.cos(angle), np.sin(angle)


def forward_table():
    c, s = cos_sin(NS, NF)
    return np.concatenate([c, s], axis=1).astype(jnp.bfloat16)


def inverse_table():
    c, s = cos_sin(NF, WIN_DEV)
    return np.concatenate([c, -s], axis=0).astype(jnp.bfloat16)


def phase_table():
    out = np.zeros((MOVE, 2, 8, LANE), np.float32)
    c, s = cos_sin(MOVE, NF)
    out[:, 0, :FB] = c.reshape(MOVE, FB, LANE)
    out[:, 1, :FB] = s.reshape(MOVE, FB, LANE)
    return out.reshape(MOVE, SLOT, LANE)


def weight_tile():
    w = np.full((NF,), 2.0 / (CH * NS), np.float32)
    w[0] = 1.0 / (CH * NS)
    out = np.zeros((8, LANE), np.float32)
    out[:FB] = w.reshape(FB, LANE)
    return out


def dot(a, b, dims=((1,), (0,))):
    return lax.dot_general(a, b, (dims, ((), ())), preferred_element_type=jnp.float32)


def plan(ids_ref, rows_ref, rank_ref, held):
    ids = ids_ref[...]
    count, lanes = ids.shape
    group = lanes // SLOTS
    per = TMPL // group
    live = ids >= 0
    livef = live.astype(jnp.float32).astype(jnp.bfloat16)
    la = lax.broadcasted_iota(jnp.int32, (lanes, lanes), 0)
    lb = lax.broadcasted_iota(jnp.int32, (lanes, lanes), 1)
    same = (la // SLOTS) == (lb // SLOTS)
    total = dot(livef, same.astype(jnp.float32).astype(jnp.bfloat16)).astype(jnp.bfloat16)
    upto = dot(livef, (same & (la <= lb)).astype(jnp.float32).astype(jnp.bfloat16))
    ra = lax.broadcasted_iota(jnp.int32, (count, count), 0)
    rb = lax.broadcasted_iota(jnp.int32, (count, count), 1)
    before = ((ra % per) == (rb % per)) & (rb < ra)
    rank = upto + dot(before.astype(jnp.float32).astype(jnp.bfloat16), total)
    rank = jnp.where(live, rank, 0.0)
    row = lax.broadcasted_iota(jnp.int32, (count, lanes), 0)
    lane = lax.broadcasted_iota(jnp.int32, (count, lanes), 1)
    column = (row % per) * group + lane // SLOTS
    place = column * held + rank.astype(jnp.int32) - 1

    slots = count // per * SLOTS
    me = lax.axis_index("tmpl")
    sa = lax.broadcasted_iota(jnp.int32, (lanes, slots), 0)
    sb = lax.broadcasted_iota(jnp.int32, (lanes, slots), 1)
    chosen = sa == (me % group) * SLOTS + (sb % SLOTS)
    mine = dot(rank.astype(jnp.bfloat16), chosen.astype(jnp.float32).astype(jnp.bfloat16))
    oa = lax.broadcasted_iota(jnp.int32, (count, slots), 0)
    ob = lax.broadcasted_iota(jnp.int32, (count, slots), 1)
    mine = jnp.where(oa == (ob // SLOTS) * per + me // group, mine, 0.0)
    rank_ref[...] = jnp.broadcast_to(jnp.sum(mine, axis=0, keepdims=True), rank_ref.shape)

    high = rows_ref.shape[0]
    hi_iota = lax.broadcasted_iota(jnp.int32, (high, lanes), 0)
    lo_iota = lax.broadcasted_iota(jnp.int32, (LANE, lanes), 0)
    hi_sum = jnp.zeros((high, LANE), jnp.float32)
    lo_sum = jnp.zeros((high, LANE), jnp.float32)
    for r in range(count):
        label = ids[r:r + 1]
        at = place[r:r + 1]
        hit = hi_iota == (label >> 7)
        hi = jnp.where(hit, (at >> 6).astype(jnp.float32), 0.0).astype(jnp.bfloat16)
        lo = jnp.where(hit, (at & 63).astype(jnp.float32), 0.0).astype(jnp.bfloat16)
        low = (lo_iota == (label & 127)).astype(jnp.float32).astype(jnp.bfloat16)
        hi_sum = hi_sum + dot(hi, low, ((1,), (1,)))
        lo_sum = lo_sum + dot(lo, low, ((1,), (1,)))
    found = hi_sum.astype(jnp.int32) * 64 + lo_sum.astype(jnp.int32)
    rows_ref[...] = jnp.clip(found, 0, TMPL * held - 1)


def sub(q):
    return q if q < FB else q + 1


JB = 2
UNROLL = 32
MESH = pl.DeviceIdType.MESH


def filtered_tiles(raw, fir, seg, filt, tile, taps_wide):
    rows = raw.shape[0]
    pieces = raw.shape[1] // SPAN
    wins = tile.shape[0] // rows
    per = pieces // wins
    taps_wide[...] = jnp.zeros_like(taps_wide)
    taps_wide[0:1, 0:NTAP] = fir[...].astype(jnp.float32)
    wide = jnp.broadcast_to(taps_wide[0:1, :], (LANE, 3 * LANE))
    band = pltpu.roll(wide, 0, 1, stride=DEC, stride_axis=0).astype(jnp.bfloat16)
    for b in range(pieces):
        here = pl.ds(b * rows, rows)
        seg[here, :SPAN] = raw[:, b * SPAN:(b + 1) * SPAN]
        if b + 1 < pieces:
            seg[here, SPAN:] = raw[:, (b + 1) * SPAN:(b + 1) * SPAN + LANE]
        else:
            seg[here, SPAN:] = jnp.zeros((rows, LANE), jnp.bfloat16)
    filt[pl.ds(0, pieces * rows), :] = dot(seg[...], band, ((1,), (1,))).astype(jnp.bfloat16)
    filt[pl.ds(pieces * rows, FB * rows), :] = jnp.zeros((FB * rows, LANE), jnp.bfloat16)
    for w in range(wins):
        for q in range(QB):
            tile[pl.ds(w * rows, rows), q * LANE:(q + 1) * LANE] = filt[
                pl.ds((w * per + q) * rows, rows), :
            ]
    values = tile[...].astype(jnp.float32)
    return lax.rsqrt(jnp.mean(values * values, axis=1, keepdims=True) + 1e-05)


def template_spectra(first, last, shift_ref, taps, head, phase, u, spread):
    count = taps.shape[2]
    many = JB * count
    turns = count // UNROLL

    def one(step, carry):
        lhs = jnp.concatenate([taps[step * JB + j].T for j in range(JB)], axis=0)
        for c in range(NS // SPAN):
            spec = dot(lhs, head[:, c * SPAN:(c + 1) * SPAN])
            for h in range(2):
                for g in range(many // 8):
                    spread[pl.ds((g * QB + 2 * c + h) * 8, 8), :] = spec[
                        g * 8:(g + 1) * 8, h * LANE:(h + 1) * LANE
                    ]

        def rows(i, inner):
            for r in range(UNROLL):
                row = i * UNROLL + r
                base = i * (UNROLL // 8 * QB * 8) + (r // 8) * QB * 8 + r % 8
                tc = spread[pl.ds(base, 8, stride=8), :]
                ts = spread[pl.ds(base + FB * 8, 8, stride=8), :]
                s = shift_ref[step * JB + i // turns, (i % turns) * UNROLL + r]
                pc = phase[s, 0:8, :]
                ps = phase[s, 8:16, :]
                u[step * many + row] = jnp.concatenate(
                    [tc * pc - ts * ps, ts * pc + tc * ps], axis=0
                ).astype(jnp.bfloat16)
            return inner

        lax.fori_loop(0, many // UNROLL, rows, 0)
        return carry

    lax.fori_loop(first, last, one, 0)


class Gather:
    def __init__(self, buf, cut, send_sem, recv_sem):
        t = lax.axis_index("tmpl")
        zl, x, c = t // 8, (t // 2) % 4, t % 2
        self.buf, self.ss, self.rs = buf, send_sem, recv_sem
        self.zl, self.x, self.zo = zl, x, 1 - zl
        self.xp, self.xm, self.x2 = lax.rem(x + 1, 4), lax.rem(x + 3, 4), lax.rem(x + 2, 4)
        self.ix = lambda a, b: (a * 4 + b) * 2 + c
        self.ox = lambda a, b: (a * 4 + b) * 2 + 1 - c
        self.up, self.down = self.ix(zl, self.xp), self.ix(zl, self.xm)
        self.over, self.beside = self.ix(self.zo, x), self.ox(zl, x)
        self.me = self.ix(zl, x)
        held = buf.shape[1]
        rest = held - cut
        self.low, self.high, self.whole = (0, cut), (cut, rest), (0, held)
        self.low1, self.low2 = (0, cut // 2), (cut // 2, cut - cut // 2)
        self.high1, self.high2 = (cut, rest // 2), (cut + rest // 2, rest - rest // 2)
        self.sends, self.last, self.wait = [], [], {}

    def copy(self, of, seg, to, k):
        ref = self.buf.at[of, pl.ds(seg[0], seg[1])]
        return pltpu.make_async_remote_copy(
            src_ref=ref, dst_ref=ref, send_sem=self.ss.at[k], recv_sem=self.rs.at[k],
            device_id={"tmpl": to}, device_id_type=MESH,
        )

    def send(self, name, of, seg, to, back):
        if seg[1]:
            k = len(self.sends)
            s = self.copy(of, seg, to, k)
            s.start()
            self.sends.append(s)
            self.wait[name] = self.copy(back, seg, to, k)

    def relay(self, a, b, seg):
        name = "beside" + str(len(self.last))
        self.send(name, self.ix(a, b), seg, self.beside, self.ox(a, b))
        if name in self.wait:
            self.last.append(self.wait[name])

    def came(self, name):
        if name in self.wait:
            self.wait[name].wait_recv()

    def start(self):
        ix, zl, zo, x, xm, xp = self.ix, self.zl, self.zo, self.x, self.xm, self.xp
        self.send("z high", self.me, self.high, self.over, ix(zo, x))
        self.send("up low", self.me, self.low, self.up, ix(zl, xm))
        self.send("down low", self.me, self.low, self.down, ix(zl, xp))
        self.send("up high", self.me, self.high, self.up, ix(zl, xm))
        self.send("down high", self.me, self.high, self.down, ix(zl, xp))
        self.send("z low", self.me, self.low, self.over, ix(zo, x))
        self.relay(zl, x, self.whole)

    def first(self):
        ix, zl, zo, x, xm, xp, x2 = self.ix, self.zl, self.zo, self.x, self.xm, self.xp, self.x2
        self.came("up low")
        self.send("up low1", ix(zl, xm), self.low1, self.up, ix(zl, x2))
        self.send("z low m", ix(zl, xm), self.low, self.over, ix(zo, xm))
        self.relay(zl, xm, self.low)
        self.came("down low")
        self.send("down low2", ix(zl, xp), self.low2, self.down, ix(zl, x2))
        self.send("z low p", ix(zl, xp), self.low, self.over, ix(zo, xp))
        self.relay(zl, xp, self.low)
        self.came("z high")
        self.send("up z", ix(zo, x), self.high, self.up, ix(zo, xm))
        self.send("down z", ix(zo, x), self.high, self.down, ix(zo, xp))
        self.relay(zo, x, self.high)

    def second(self):
        ix, zl, zo, x, xm, xp, x2 = self.ix, self.zl, self.zo, self.x, self.xm, self.xp, self.x2
        self.came("up high")
        self.send("up high1", ix(zl, xm), self.high1, self.up, ix(zl, x2))
        self.relay(zl, xm, self.high)
        self.came("down high")
        self.send("down high2", ix(zl, xp), self.high2, self.down, ix(zl, x2))
        self.relay(zl, xp, self.high)
        self.came("z low")
        self.relay(zo, x, self.low)

    def third(self):
        ix, zl, zo, xm, xp, x2 = self.ix, self.zl, self.zo, self.xm, self.xp, self.x2
        self.came("up low1")
        self.send("z low1", ix(zl, x2), self.low1, self.over, ix(zo, x2))
        self.relay(zl, x2, self.low1)
        self.came("down low2")
        self.send("z low2", ix(zl, x2), self.low2, self.over, ix(zo, x2))
        self.relay(zl, x2, self.low2)
        self.came("up z")
        self.send("up z1", ix(zo, xm), self.high1, self.up, ix(zo, x2))
        self.relay(zo, xm, self.high)
        self.came("down z")
        self.send("down z2", ix(zo, xp), self.high2, self.down, ix(zo, x2))
        self.relay(zo, xp, self.high)

    def fourth(self):
        for name, a, b, seg in (
            ("z low m", self.zo, self.xm, self.low), ("z low p", self.zo, self.xp, self.low),
            ("up high1", self.zl, self.x2, self.high1), ("down high2", self.zl, self.x2, self.high2),
        ):
            self.came(name)
            self.relay(a, b, seg)

    def finish(self):
        for name, a, b, seg in (
            ("z low1", self.zo, self.x2, self.low1), ("z low2", self.zo, self.x2, self.low2),
            ("up z1", self.zo, self.x2, self.high1), ("down z2", self.zo, self.x2, self.high2),
        ):
            self.came(name)
            self.relay(a, b, seg)
        for r in self.last:
            r.wait_recv()

    def drain(self):
        for s in self.sends:
            s.wait_send()


def match_kernel(
    wins,
    raw_hbm, fir_hbm, ids_hbm, chan_hbm, shift_hbm, taps_hbm, table_hbm, head_hbm, phase_hbm,
    weight_hbm, inverse_hbm,
    out_ref,
    raw, fir, ids, chan, shift, taps, table, head, phase, weight, inverse,
    fir_wide, seg, filt, tile, rank, rows_v, rows, spec, mine, wide, buf_c, buf_s, u, spread, z,
    packed, fetch_sem, a_send, a_recv, b_send, b_recv, c_send, c_recv, s_send, s_recv,
):
    slots = raw.shape[0]
    w = lax.axis_index("win")
    t = lax.axis_index("tmpl")
    held = buf_c.shape[1]
    moves_of = ((a_send, a_recv), (b_send, b_recv))
    bufs = (buf_c, buf_s)
    gathers = (
        Gather(buf_c, CUT_C, c_send, c_recv), Gather(buf_s, CUT_S, s_send, s_recv)
    )

    barrier = pltpu.get_barrier_semaphore()
    for d in range(1, wins):
        pl.semaphore_signal(
            barrier, inc=1, device_id={"win": lax.rem(w + d, wins)}, device_id_type=MESH
        )
    g = gathers[0]
    for d in (g.up, g.down, g.over, g.beside):
        pl.semaphore_signal(barrier, inc=1, device_id={"tmpl": d}, device_id_type=MESH)

    pairs = (
        (raw_hbm, raw), (fir_hbm, fir), (ids_hbm, ids), (table_hbm, table), (shift_hbm, shift),
        (chan_hbm, chan), (taps_hbm, taps), (head_hbm, head), (phase_hbm, phase),
        (weight_hbm, weight), (inverse_hbm, inverse),
    )
    fetches = [
        pltpu.make_async_copy(a, b, fetch_sem.at[i]) for i, (a, b) in enumerate(pairs)
    ]
    for f in fetches:
        f.start()

    fetches[0].wait()
    fetches[1].wait()
    scale = filtered_tiles(raw, fir, seg, filt, tile, fir_wide)
    fetches[3].wait()

    def block(ref, half, i):
        return ref.at[half, pl.ds(pl.multiple_of(i * slots, slots), slots)]

    own = pl.ds(pl.multiple_of(w * slots, slots), slots)
    moves = ([], [])
    for half in range(2):
        spec[half] = (dot(tile[...], table[:, half * NF:(half + 1) * NF]) * scale).astype(
            jnp.bfloat16
        )
        if half == 0:
            pl.semaphore_wait(barrier, wins + 3)
        for d in range(1, wins):
            to = lax.rem(w + d, wins)
            move = pltpu.make_async_remote_copy(
                src_ref=block(spec, half, to), dst_ref=block(mine, half, w),
                send_sem=moves_of[half][0].at[d - 1], recv_sem=moves_of[half][1].at[d - 1],
                device_id={"win": to}, device_id_type=MESH,
            )
            move.start()
            moves[half].append(move)
        mine[half, own, :] = spec[half, own, :]

    fetches[2].wait()
    plan(ids, rows_v, rank, held)
    table_out = pltpu.make_async_copy(rows_v, rows, fetch_sem.at[len(pairs)])
    table_out.start()
    for f in fetches[4:9]:
        f.wait()

    def templates(first, last):
        template_spectra(first, last, shift, taps, head, phase, u, spread)

    tall = wide.shape[0] // 8

    def compact(half):
        for move in moves[half]:
            move.wait_recv()
        order = lax.broadcasted_iota(jnp.int32, (tall, mine.shape[1]), 0).astype(jnp.float32) + 1.0
        pick = (order == rank[0:1, :]).astype(jnp.float32).astype(jnp.bfloat16)
        part = dot(pick, mine[half])
        for q in range(FB):
            for i in range(tall // 8):
                wide[pl.ds(i * 64 + q, 8, stride=8), :] = part[
                    i * 8:(i + 1) * 8, q * LANE:(q + 1) * LANE
                ]
        for i in range(held):
            bufs[half][t, i] = wide[pl.ds(i * 8, 8), :].astype(jnp.bfloat16)

    count = chan.shape[1]
    flats = [b.reshape(b.shape[0] * held, 8, LANE) for b in bufs]

    def template(half, k):
        zr = [jnp.zeros((8, LANE), jnp.float32)] * 2
        zi = [jnp.zeros((8, LANE), jnp.float32)] * 2
        for j in range(CH):
            name = chan[j, k]
            xv = flats[half][rows[name >> 7, name & 127]].astype(jnp.float32)
            uv = u[j * count + k].astype(jnp.float32)
            ur, ui = uv[:8], uv[8:]
            a = j % 2
            if half == 0:
                zr[a] = zr[a] + ur * xv
                zi[a] = zi[a] + ui * xv
            else:
                zr[a] = zr[a] + ui * xv
                zi[a] = zi[a] - ur * xv
        at = pl.ds(pl.multiple_of(k * SLOT, SLOT), 8)
        more = pl.ds(pl.multiple_of(k * SLOT + 8, 8), 8)
        if half == 0:
            z[at, :] = zr[0] + zr[1]
            z[more, :] = zi[0] + zi[1]
        else:
            z[at, :] = (z[at, :] + (zr[0] + zr[1])) * weight[...]
            z[more, :] = (z[more, :] + (zi[0] + zi[1])) * weight[...]

    def stack(half, first, last):
        def two(i, carry):
            template(half, 2 * i)
            template(half, 2 * i + 1)
            return carry

        lax.fori_loop(first // 2, last // 2, two, 0)

    c, s = gathers
    q4 = count // 4
    templates(0, 5)
    table_out.wait()
    compact(0)
    c.start()
    templates(5, 7)
    c.first()
    templates(7, 8)
    c.second()
    templates(8, 10)
    compact(1)
    s.start()
    templates(10, 12)
    c.third()
    templates(12, 13)
    s.first()
    c.fourth()
    templates(13, 15)
    s.second()
    c.finish()
    for f in fetches[9:]:
        f.wait()
    stack(0, 0, q4)
    s.third()
    stack(0, q4, 2 * q4)
    s.fourth()
    stack(0, 2 * q4, 4 * q4)
    s.finish()
    stack(1, 0, count)
    for q in range(QB):
        for i in range(count // 16):
            halves = [
                z[pl.ds((i * 16 + 8 * h) * SLOT + sub(q), 8, stride=SLOT), :] for h in range(2)
            ]
            packed[pl.ds(i * 16, 16), q * LANE:(q + 1) * LANE] = jnp.concatenate(
                halves, axis=0
            ).astype(jnp.bfloat16)
    out_ref[...] = dot(packed[...], inverse[...])

    for half in range(2):
        for move in moves[half]:
            move.wait_send()
        gathers[half].drain()


def matched(raw, fir, ids, channels, shifts, taps, wins, tmpls, held):
    count = taps.shape[2]
    slots, length = raw.shape
    pieces = length // SPAN
    high = -(-held * tmpls // (8 * LANE)) * 8
    tall = -(-held // 16) * 16
    forward = forward_table()
    args = (
        raw, fir.reshape(1, -1), ids.reshape(-1, LANE), channels, shifts, taps,
        jnp.asarray(forward), jnp.asarray(forward[:TL]), jnp.asarray(phase_table()),
        jnp.asarray(weight_tile()), jnp.asarray(inverse_table()),
    )
    smem = (3, 4)
    staged = [
        (pltpu.SMEM if i in smem else pltpu.VMEM)(a.shape, a.dtype) for i, a in enumerate(args)
    ]
    dma = pltpu.SemaphoreType.DMA
    return pl.pallas_call(
        functools.partial(match_kernel, wins),
        out_shape=jax.ShapeDtypeStruct((count, WIN_DEV), jnp.float32),
        in_specs=[pl.BlockSpec(memory_space=pl.ANY)] * len(args),
        out_specs=pl.BlockSpec(memory_space=pltpu.VMEM),
        scratch_shapes=staged + [
            pltpu.VMEM((8, 3 * LANE), jnp.float32),
            pltpu.VMEM((pieces * slots, 3 * LANE), jnp.bfloat16),
            pltpu.VMEM(((pieces + FB) * slots, LANE), jnp.bfloat16),
            pltpu.VMEM((wins * slots, NS), jnp.bfloat16),
            pltpu.VMEM((8, wins * slots), jnp.float32),
            pltpu.VMEM((high, LANE), jnp.int32),
            pltpu.SMEM((high, LANE), jnp.int32),
            pltpu.VMEM((2, wins * slots, NF), jnp.bfloat16),
            pltpu.VMEM((2, wins * slots, NF), jnp.bfloat16),
            pltpu.VMEM((tall * 8, LANE), jnp.float32),
            pltpu.VMEM((tmpls, held, 8, LANE), jnp.bfloat16),
            pltpu.VMEM((tmpls, held, 8, LANE), jnp.bfloat16),
            pltpu.VMEM((count * CH, SLOT, LANE), jnp.bfloat16),
            pltpu.VMEM((JB * count * SLOT, LANE), jnp.float32),
            pltpu.VMEM((count * SLOT, LANE), jnp.float32),
            pltpu.VMEM((count, NS), jnp.bfloat16),
            dma((len(args) + 1,)),
            dma((wins - 1,)), dma((wins - 1,)), dma((wins - 1,)), dma((wins - 1,)),
            dma((37,)), dma((37,)), dma((37,)), dma((37,)),
        ],
        compiler_params=pltpu.CompilerParams(
            vmem_limit_bytes=62 * MIB, collective_id=0, has_side_effects=True
        ),
        name="matched",
    )(*args)


def on_device(raw, ids, fir, taps, channels, shifts):
    wins = lax.axis_size("win")
    tmpls = lax.axis_size("tmpl")
    held = 3 * SLOTS * wins // 5
    return matched(
        raw, fir, ids, channels.T, shifts.T, jnp.transpose(taps, (1, 2, 0)), wins, tmpls, held
    )


def solution(mesh):
    return jax.shard_map(
        on_device,
        mesh=mesh,
        in_specs=(
            P(("win", "tmpl"), None),
            P(),
            P(),
            P("tmpl", None, None),
            P("tmpl", None),
            P("tmpl", None),
        ),
        out_specs=P("tmpl", "win"),
        check_vma=False,
    )
```

time: 105 us -> 99.6 us (0.949)
  local copies, waits for them, and re-layouts: 8.78 us -> 1.89 us
  Pallas kernels: 95 us -> 97.6 us
    unnamed x13 -> x1, local copies, waits for them, and re-layouts: 8.78 us -> 1.89 us
    pallas_call x2 -> x1, Pallas kernels: 95 us -> 97.6 us  [matched(): pl.pallas_call(functools.partial(match_kernel, wins), out_shape=jax.Shape...]
where the time goes in v3:
time: 99.6 us; the launch traced here: 99.5 us
  Pallas kernels  97.6 us (98%)
  local copies, waits for them, and re-layouts  1.89 us (2%)
    pallas_call x1, Pallas kernels, matched(): pl.pallas_call(functools.partial(match_kernel, wins), out_shape=jax.Shape...  97.6 us

profile of v3, /device:TPU:1, one launch (start us, length us, event | category | flops | bytes accessed | tf_op | source)
XLA Modules:
  0.0 99.5 jit_solution(10843876487998186081)
XLA Ops:
  0.0 97.6 %matched.1 = f32[128,1024]{1,0:T(8,128)} custom-call(bf16[16,32768]{1,0:T(8,128)(2,1)} %raw_hbm.1, bf16[1,64]{1,0:T(2,128)(2,1)} %bitcast.9, s32[32,128]{1,0:T(8,128)} %bitcast.6, s32[30,128]{1,0:T(8,128)} %bitcast.7, s32[30,128]{1,0:T(8,128)} %bitcast.8, bf16[30,400,128]{2,1,0:T(8,128)(2,1)} %bitcast.5, bf16[1792,1792]{1,0:T(8,128)(2,1)} %constant.10.clone.table_hbm, ...), custom_call_target="tpu_custom_call" | custom-call | tf_op jit(solution)/shard_map/matched/pallas_call | solution.py:497
  97.6 1.9 %copy.13 = f32[128,1024]{1,0:T(8,128)} copy(f32[128,1024]{1,0:T(8,128)} %matched.1) | data formatting | bytes 1048576

commit v4 on v3

--- a/solution.py
+++ b/solution.py
@@ -24,7 +24,7 @@
 SPAN = DEC * LANE
 SLOTS = 16
 TMPL = 16
-CUT_C = 0
+CUT_C = 61
 CUT_S = 61
 MIB = 1 << 20
 
@@ -64,7 +64,7 @@
     return lax.dot_general(a, b, (dims, ((), ())), preferred_element_type=jnp.float32)
 
 
-def plan(ids_ref, rows_ref, rank_ref, held):
+def plan(ids_ref, chan_ref, index_ref, rank_ref, held, high):
     ids = ids_ref[...]
     count, lanes = ids.shape
     group = lanes // SLOTS
@@ -97,7 +97,6 @@
     mine = jnp.where(oa == (ob // SLOTS) * per + me // group, mine, 0.0)
     rank_ref[...] = jnp.broadcast_to(jnp.sum(mine, axis=0, keepdims=True), rank_ref.shape)
 
-    high = rows_ref.shape[0]
     hi_iota = lax.broadcasted_iota(jnp.int32, (high, lanes), 0)
     lo_iota = lax.broadcasted_iota(jnp.int32, (LANE, lanes), 0)
     hi_sum = jnp.zeros((high, LANE), jnp.float32)
@@ -111,8 +110,16 @@
         low = (lo_iota == (label & 127)).astype(jnp.float32).astype(jnp.bfloat16)
         hi_sum = hi_sum + dot(hi, low, ((1,), (1,)))
         lo_sum = lo_sum + dot(lo, low, ((1,), (1,)))
-    found = hi_sum.astype(jnp.int32) * 64 + lo_sum.astype(jnp.int32)
-    rows_ref[...] = jnp.clip(found, 0, TMPL * held - 1)
+    both = jnp.concatenate([hi_sum, lo_sum], axis=0).astype(jnp.bfloat16)
+    for j in range(chan_ref.shape[0]):
+        name = chan_ref[j:j + 1, :]
+        low = (lo_iota == (name & 127)).astype(jnp.float32).astype(jnp.bfloat16)
+        got = dot(both, low)
+        hit = hi_iota == (name >> 7)
+        hi = jnp.sum(jnp.where(hit, got[:high], 0.0), axis=0, keepdims=True)
+        lo = jnp.sum(jnp.where(hit, got[high:], 0.0), axis=0, keepdims=True)
+        found = hi.astype(jnp.int32) * 64 + lo.astype(jnp.int32)
+        index_ref[j:j + 1, :] = jnp.clip(found, 0, TMPL * held - 1)
 
 
 def sub(q):
@@ -310,7 +317,7 @@
     weight_hbm, inverse_hbm,
     out_ref,
     raw, fir, ids, chan, shift, taps, table, head, phase, weight, inverse,
-    fir_wide, seg, filt, tile, rank, rows_v, rows, spec, mine, wide, buf_c, buf_s, u, spread, z,
+    fir_wide, seg, filt, tile, rank, index_v, index, spec, mine, wide, buf_c, buf_s, u, spread, z,
     packed, fetch_sem, a_send, a_recv, b_send, b_recv, c_send, c_recv, s_send, s_recv,
 ):
     slots = raw.shape[0]
@@ -333,20 +340,20 @@
         pl.semaphore_signal(barrier, inc=1, device_id={"tmpl": d}, device_id_type=MESH)
 
     pairs = (
-        (raw_hbm, raw), (fir_hbm, fir), (ids_hbm, ids), (table_hbm, table), (shift_hbm, shift),
-        (chan_hbm, chan), (taps_hbm, taps), (head_hbm, head), (phase_hbm, phase),
+        (raw_hbm, raw), (fir_hbm, fir), (table_hbm.at[0], table.at[0]),
+        (table_hbm.at[1], table.at[1]), (ids_hbm, ids), (chan_hbm, chan), (shift_hbm, shift),
+        (taps_hbm, taps), (head_hbm, head), (phase_hbm, phase),
         (weight_hbm, weight), (inverse_hbm, inverse),
     )
     fetches = [
         pltpu.make_async_copy(a, b, fetch_sem.at[i]) for i, (a, b) in enumerate(pairs)
     ]
-    for f in fetches:
+    for f in fetches[:7]:
         f.start()
 
     fetches[0].wait()
     fetches[1].wait()
     scale = filtered_tiles(raw, fir, seg, filt, tile, fir_wide)
-    fetches[3].wait()
 
     def block(ref, half, i):
         return ref.at[half, pl.ds(pl.multiple_of(i * slots, slots), slots)]
@@ -354,7 +361,8 @@
     own = pl.ds(pl.multiple_of(w * slots, slots), slots)
     moves = ([], [])
     for half in range(2):
-        spec[half] = (dot(tile[...], table[:, half * NF:(half + 1) * NF]) * scale).astype(
+        fetches[2 + half].wait()
+        spec[half] = (dot(tile[...], table[half]) * scale).astype(
             jnp.bfloat16
         )
         if half == 0:
@@ -370,11 +378,14 @@
             moves[half].append(move)
         mine[half, own, :] = spec[half, own, :]
 
-    fetches[2].wait()
-    plan(ids, rows_v, rank, held)
-    table_out = pltpu.make_async_copy(rows_v, rows, fetch_sem.at[len(pairs)])
+    for f in fetches[7:]:
+        f.start()
+    fetches[4].wait()
+    fetches[5].wait()
+    plan(ids, chan, index_v, rank, held, -(-held * TMPL // (8 * LANE)) * 8)
+    table_out = pltpu.make_async_copy(index_v, index, fetch_sem.at[len(pairs)])
     table_out.start()
-    for f in fetches[4:9]:
+    for f in fetches[6:10]:
         f.wait()
 
     def templates(first, last):
@@ -403,8 +414,7 @@
         zr = [jnp.zeros((8, LANE), jnp.float32)] * 2
         zi = [jnp.zeros((8, LANE), jnp.float32)] * 2
         for j in range(CH):
-            name = chan[j, k]
-            xv = flats[half][rows[name >> 7, name & 127]].astype(jnp.float32)
+            xv = flats[half][index[j, k]].astype(jnp.float32)
             uv = u[j * count + k].astype(jnp.float32)
             ur, ui = uv[:8], uv[8:]
             a = j % 2
@@ -452,7 +462,7 @@
     templates(13, 15)
     s.second()
     c.finish()
-    for f in fetches[9:]:
+    for f in fetches[10:]:
         f.wait()
     stack(0, 0, q4)
     s.third()
@@ -481,15 +491,14 @@
     count = taps.shape[2]
     slots, length = raw.shape
     pieces = length // SPAN
-    high = -(-held * tmpls // (8 * LANE)) * 8
     tall = -(-held // 16) * 16
     forward = forward_table()
     args = (
         raw, fir.reshape(1, -1), ids.reshape(-1, LANE), channels, shifts, taps,
-        jnp.asarray(forward), jnp.asarray(forward[:TL]), jnp.asarray(phase_table()),
+        jnp.asarray(np.stack([forward[:, :NF], forward[:, NF:]])), jnp.asarray(forward[:TL]), jnp.asarray(phase_table()),
         jnp.asarray(weight_tile()), jnp.asarray(inverse_table()),
     )
-    smem = (3, 4)
+    smem = (4,)
     staged = [
         (pltpu.SMEM if i in smem else pltpu.VMEM)(a.shape, a.dtype) for i, a in enumerate(args)
     ]
@@ -505,8 +514,8 @@
             pltpu.VMEM(((pieces + FB) * slots, LANE), jnp.bfloat16),
             pltpu.VMEM((wins * slots, NS), jnp.bfloat16),
             pltpu.VMEM((8, wins * slots), jnp.float32),
-            pltpu.VMEM((high, LANE), jnp.int32),
-            pltpu.SMEM((high, LANE), jnp.int32),
+            pltpu.VMEM(channels.shape, jnp.int32),
+            pltpu.SMEM(channels.shape, jnp.int32),
             pltpu.VMEM((2, wins * slots, NF), jnp.bfloat16),
             pltpu.VMEM((2, wins * slots, NF), jnp.bfloat16),
             pltpu.VMEM((tall * 8, LANE), jnp.float32),
@@ -516,7 +525,7 @@
             pltpu.VMEM((JB * count * SLOT, LANE), jnp.float32),
             pltpu.VMEM((count * SLOT, LANE), jnp.float32),
             pltpu.VMEM((count, NS), jnp.bfloat16),
-            dma((len(args) + 1,)),
+            dma((len(args) + 2,)),
             dma((wins - 1,)), dma((wins - 1,)), dma((wins - 1,)), dma((wins - 1,)),
             dma((37,)), dma((37,)), dma((37,)), dma((37,)),
         ],

time: 99.6 us -> 77.8 us (0.78)
  Pallas kernels: 97.6 us -> 75.8 us
    pallas_call x1, Pallas kernels: 97.6 us -> 75.8 us  [matched(): pl.pallas_call(functools.partial(match_kernel, wins), out_shape=jax.Shape...]
where the time goes in v4:
time: 77.8 us; the launch traced here: 77.7 us
  Pallas kernels  75.8 us (97%)
  local copies, waits for them, and re-layouts  1.89 us (2%)
    pallas_call x1, Pallas kernels, matched(): pl.pallas_call(functools.partial(match_kernel, wins), out_shape=jax.Shape...  75.8 us
    unnamed x1, local copies, waits for them, and re-layouts  1.89 us

profile of v4, /device:TPU:1, one launch (start us, length us, event | category | flops | bytes accessed | tf_op | source)
XLA Modules:
  0.0 77.7 jit_solution(16455387103131635662)
XLA Ops:
  0.0 75.8 %matched.1 = f32[128,1024]{1,0:T(8,128)} custom-call(bf16[16,32768]{1,0:T(8,128)(2,1)} %raw_hbm.1, bf16[1,64]{1,0:T(2,128)(2,1)} %bitcast.9, s32[32,128]{1,0:T(8,128)} %bitcast.6, s32[30,128]{1,0:T(8,128)} %bitcast.7, s32[30,128]{1,0:T(8,128)} %bitcast.8, bf16[30,400,128]{2,1,0:T(8,128)(2,1)} %bitcast.5, bf16[2,1792,896]{2,1,0:T(8,128)(2,1)} %constant.10.clone.table_hbm, ...), custom_call_target="tpu_custom_call" | custom-call | tf_op jit(solution)/shard_map/matched/pallas_call | solution.py:506
  75.8 1.9 %copy.13 = f32[128,1024]{1,0:T(8,128)} copy(f32[128,1024]{1,0:T(8,128)} %matched.1) | data formatting | bytes 1048576

commit v5 on v4

--- a/solution.py
+++ b/solution.py
@@ -360,13 +360,12 @@
 
     own = pl.ds(pl.multiple_of(w * slots, slots), slots)
     moves = ([], [])
-    for half in range(2):
+
+    def transform(half):
         fetches[2 + half].wait()
-        spec[half] = (dot(tile[...], table[half]) * scale).astype(
-            jnp.bfloat16
-        )
-        if half == 0:
-            pl.semaphore_wait(barrier, wins + 3)
+        spec[half] = (dot(tile[...], table[half]) * scale).astype(jnp.bfloat16)
+
+    def spread_rows(half):
         for d in range(1, wins):
             to = lax.rem(w + d, wins)
             move = pltpu.make_async_remote_copy(
@@ -378,6 +377,10 @@
             moves[half].append(move)
         mine[half, own, :] = spec[half, own, :]
 
+    transform(0)
+    pl.semaphore_wait(barrier, wins + 3)
+    spread_rows(0)
+    transform(1)
     for f in fetches[7:]:
         f.start()
     fetches[4].wait()
@@ -443,32 +446,33 @@
 
     c, s = gathers
     q4 = count // 4
-    templates(0, 5)
+    templates(0,3)
     table_out.wait()
     compact(0)
     c.start()
-    templates(5, 7)
+    spread_rows(1)
+    templates(3,5)
     c.first()
-    templates(7, 8)
+    templates(5,7)
     c.second()
-    templates(8, 10)
+    templates(7,9)
     compact(1)
     s.start()
-    templates(10, 12)
+    templates(9,11)
     c.third()
-    templates(12, 13)
+    templates(11,12)
     s.first()
     c.fourth()
-    templates(13, 15)
+    templates(12,15)
     s.second()
     c.finish()
     for f in fetches[10:]:
         f.wait()
-    stack(0, 0, q4)
+    stack(0,0,q4)
     s.third()
-    stack(0, q4, 2 * q4)
+    stack(0,q4,2*q4)
     s.fourth()
-    stack(0, 2 * q4, 4 * q4)
+    stack(0,2*q4,4*q4)
     s.finish()
     stack(1, 0, count)
     for q in range(QB):

time: 77.8 us -> 76.5 us (0.983); the launches traced: 77.7 us -> 75.3 us
  Pallas kernels: 75.8 us -> 73.4 us
    pallas_call x1, Pallas kernels: 75.8 us -> 73.4 us  [matched(): pl.pallas_call(functools.partial(match_kernel, wins), out_shape=jax.Shape...]
where the time goes in v5:
time: 76.5 us; the launch traced here: 75.3 us
  Pallas kernels  73.4 us (96%)
  local copies, waits for them, and re-layouts  1.89 us (2%)
    pallas_call x1, Pallas kernels, matched(): pl.pallas_call(functools.partial(match_kernel, wins), out_shape=jax.Shape...  73.4 us
    unnamed x1, local copies, waits for them, and re-layouts  1.89 us

profile of v5, /device:TPU:1, one launch (start us, length us, event | category | flops | bytes accessed | tf_op | source)
XLA Modules:
  0.0 75.3 jit_solution(6600777180568195895)
XLA Ops:
  0.0 73.4 %matched.1 = f32[128,1024]{1,0:T(8,128)} custom-call(bf16[16,32768]{1,0:T(8,128)(2,1)} %raw_hbm.1, bf16[1,64]{1,0:T(2,128)(2,1)} %bitcast.9, s32[32,128]{1,0:T(8,128)} %bitcast.6, s32[30,128]{1,0:T(8,128)} %bitcast.7, s32[30,128]{1,0:T(8,128)} %bitcast.8, bf16[30,400,128]{2,1,0:T(8,128)(2,1)} %bitcast.5, bf16[2,1792,896]{2,1,0:T(8,128)(2,1)} %constant.10.clone.table_hbm, ...), custom_call_target="tpu_custom_call" | custom-call | tf_op jit(solution)/shard_map/matched/pallas_call | solution.py:510
  73.4 1.9 %copy.13 = f32[128,1024]{1,0:T(8,128)} copy(f32[128,1024]{1,0:T(8,128)} %matched.1) | data formatting | bytes 1048576

commit v6 on v5

--- a/solution.py
+++ b/solution.py
@@ -437,12 +437,12 @@
             z[more, :] = (z[more, :] + (zi[0] + zi[1])) * weight[...]
 
     def stack(half, first, last):
-        def two(i, carry):
-            template(half, 2 * i)
-            template(half, 2 * i + 1)
+        def four(i, carry):
+            for k in range(4):
+                template(half, 4 * i + k)
             return carry
 
-        lax.fori_loop(first // 2, last // 2, two, 0)
+        lax.fori_loop(first // 4, last // 4, four, 0)
 
     c, s = gathers
     q4 = count // 4

time: 76.5 us -> 76.1 us (level)
  no operation moved by 1% of the time
where the time goes in v6:
time: 76.1 us; the launch traced here: 74.8 us
  Pallas kernels  73 us (96%)
  local copies, waits for them, and re-layouts  1.89 us (2%)
    pallas_call x1, Pallas kernels, matched(): pl.pallas_call(functools.partial(match_kernel, wins), out_shape=jax.Shape...  73 us
    unnamed x1, local copies, waits for them, and re-layouts  1.89 us

profile of v6, /device:TPU:1, one launch (start us, length us, event | category | flops | bytes accessed | tf_op | source)
XLA Modules:
  0.0 74.8 jit_solution(1919783538974671060)
XLA Ops:
  0.0 73.0 %matched.1 = f32[128,1024]{1,0:T(8,128)} custom-call(bf16[16,32768]{1,0:T(8,128)(2,1)} %raw_hbm.1, bf16[1,64]{1,0:T(2,128)(2,1)} %bitcast.9, s32[32,128]{1,0:T(8,128)} %bitcast.6, s32[30,128]{1,0:T(8,128)} %bitcast.7, s32[30,128]{1,0:T(8,128)} %bitcast.8, bf16[30,400,128]{2,1,0:T(8,128)(2,1)} %bitcast.5, bf16[2,1792,896]{2,1,0:T(8,128)(2,1)} %constant.10.clone.table_hbm, ...), custom_call_target="tpu_custom_call" | custom-call | tf_op jit(solution)/shard_map/matched/pallas_call | solution.py:510
  73.0 1.9 %copy.13 = f32[128,1024]{1,0:T(8,128)} copy(f32[128,1024]{1,0:T(8,128)} %matched.1) | data formatting | bytes 1048576
